TPU v7x, 512 devices: a whole 4x8x8 slice. The times are simulated.
512 devices in a mesh: node: 128 (over z, y, core), feat: 4 (over x).
Axes of the slice: x: 4, y: 8, z: 8, core: 2. Of those that a mesh axis runs over, the one named last changes fastest.
Arguments:
- embed: bfloat16 [256, 131072], P('feat', 'node'), may hold values from -6 to 6
- tile_weight: bfloat16 [128, 135, 128, 128], P('node'), may hold values from -0.125 to 0.125
- tile_rows: int32 [128, 135], P('node'), may hold values from 0 to 7
- tile_cols: int32 [128, 135], P('node'), may hold values from 0 to 135, as said below
- send_rows: int32 [128, 128], P('node'), may hold values from 0 to 7
- src_local: int32 [65536], P('node'), may hold values from 0 to 1023
- dst_owner: int32 [65536, 1], P('node'), may hold values from 0 to 127; in each aligned block of 512 rows (0 to 511, 512 to 1023, ...) at most 8 rows name the same one
- dst_local: int32 [65536], P('node'), may hold values from 0 to 1023
- w_in: bfloat16 [256, 1024], P('feat'), may hold values from -0.375 to 0.375
- b_in: float32 [1024], replicated, may hold values from -4 to 4
- w_out: float32 [1024], replicated, may hold values from -0.1875 to 0.1875
Outputs:
- propagated: bfloat16 [256, 131072], P('feat', 'node')
- scores: float32 [65536], P('node')
Inputs may be any that keep to these rules, and one draw needn't show every extreme that they name: In each part, the entries of tile_cols below 8 are the numbers 0 to 7 once each, and tile_rows equals tile_cols at those tiles; the other 127 entries are 8 + p for every part p other than the part itself, once each. `dst_owner`: among the 512 queries of one part, at most 8 have the same destination part, and exactly 8 do for some destination part.
All inputs are finite; a program needn't handle non-finite values.
Results may differ from a plain program's by a relative error of at most 0.015.
Values may be sent and summed in bfloat16 or wider, within the bound.
A program may use at most 64 MiB of HBM per device.

v0:
```python
import jax
import jax.numpy as jnp
from jax import lax
from jax.sharding import PartitionSpec as P

HOPS = 2


TELEPORT = 0.1


def propagate(current, initial, weights, tile_row, tile_col, targets):
    channels, node_count = current.shape
    block_size = weights.shape[-1]
    block_count = node_count // block_size
    blocked = current.reshape(channels, block_count, block_size)
    outgoing = blocked[:, targets, :]
    incoming = lax.all_to_all(outgoing, "node", split_axis=1, concat_axis=1, tiled=True)
    sources = jnp.concatenate([blocked, incoming], axis=1)
    picked = sources[:, tile_col, :]
    products = jnp.einsum("ctj,tij->cti", picked, weights, preferred_element_type=jnp.float32)
    selector = (tile_row[None, :] == jnp.arange(block_count, dtype=jnp.int32)[:, None]).astype(
        jnp.float32
    )
    summed = jnp.einsum("rt,cti->cri", selector, products, precision=lax.Precision.HIGHEST)
    return ((1.0 - TELEPORT) * summed.reshape(channels, node_count) + TELEPORT * initial).astype(
        jnp.bfloat16
    )


def contract_rows(left_matrix, right_matrix):
    return lax.dot_general(
        left_matrix, right_matrix, (((0,), (0,)), ((), ())), preferred_element_type=jnp.float32
    )


def shards(
    embed,
    tile_weight,
    tile_rows,
    tile_cols,
    send_rows,
    src_local,
    dst_owner,
    dst_local,
    w_in,
    b_in,
    w_out,
):
    weights = tile_weight[0]
    tile_row = tile_rows[0]
    tile_col = tile_cols[0]
    targets = send_rows[0]
    initial = embed.astype(jnp.float32)
    current = embed
    for hop_index in range(HOPS):
        current = propagate(current, initial, weights, tile_row, tile_col, targets)
    part_count = lax.axis_size("node")
    queries = src_local.shape[0]
    capacity = max(2, 2 * queries // part_count)
    owners = dst_owner[:, 0]
    owner_hits = (owners[:, None] == jnp.arange(part_count, dtype=jnp.int32)[None, :]).astype(
        jnp.int32
    )
    slot_rank = jnp.sum(jnp.cumsum(owner_hits, axis=0) * owner_hits, axis=1) - 1
    requests = (
        jnp.zeros((part_count * capacity,), jnp.int32)
        .at[owners * capacity + slot_rank]
        .set(dst_local)
    )
    requests = requests.reshape(part_count, capacity)
    replies = lax.all_to_all(
        current[:, lax.all_to_all(requests, "node", split_axis=0, concat_axis=0, tiled=True)],
        "node",
        split_axis=1,
        concat_axis=1,
        tiled=True,
    )
    target_rows = replies[:, owners, slot_rank]
    source_rows = current[:, src_local]
    hadamard = (source_rows.astype(jnp.float32) * target_rows.astype(jnp.float32)).astype(
        jnp.bfloat16
    )
    partial_value = contract_rows(w_in, hadamard)
    hidden = lax.psum(partial_value.astype(jnp.bfloat16), "feat").astype(jnp.float32)
    active = jnp.maximum(hidden + b_in[:, None], 0.0)
    scores = jnp.dot(w_out, active, precision=lax.Precision.HIGHEST)
    return (current, scores)


def solution(mesh):
    placed = (
        P("feat", "node"),
        P("node", None, None, None),
        P("node", None),
        P("node", None),
        P("node", None),
        P("node"),
        P("node", None),
        P("node"),
        P("feat", None),
        P(),
        P(),
    )
    return jax.shard_map(
        shards,
        mesh=mesh,
        in_specs=placed,
        out_specs=(P("feat", "node"), P("node")),
        check_vma=False,
    )
```

profile of v0, /device:TPU:1, one launch (start us, length us, event | category | flops | bytes accessed | tf_op | source)
XLA Modules:
  0.0 273.3 jit_solution(4774526276266268185)
XLA Ops:
  7.2 0.0 copy-start
  7.2 1.0 copy_bitcast_fusion
  8.1 0.7 fusion.56
  8.8 2.2 gather_fusion
  11.0 0.0 copy-start.1
  11.0 0.0 copy-start.2
  11.0 0.0 copy-start.5
  11.0 18.6 %all-to-all-start = ((bf16[64,128,128]{2,0,1:T(8,128)(2,1)}), bf16[64,128,128]{2,0,1:T(8,128)(2,1)S(1)}, u32[]{:S(2)}, u32[]{:S(2)}) async-start(bf16[64,128,128]{2,0,1:T(8,128)(2,1)} %bitcast.90), calls=%async_computation | async-start | bytes 4194304 | tf_op jit(solution)/shard_map/all_to_all | solution.py:18
  29.5 0.0 copy-done.1
  29.6 0.2 copy.72
  29.7 0.0 copy-done.2
  29.7 0.1 copy.79
  29.9 0.2 fusion.42
  30.2 0.2 fusion.41
  30.4 2.6 scatter_custom_fusion
  33.0 0.7 all_to_all.19
  33.8 0.0 copy-done.5
  33.8 47.0 %all-to-all-done = bf16[64,128,128]{2,0,1:T(8,128)(2,1)S(1)} async-done(((bf16[64,128,128]{2,0,1:T(8,128)(2,1)}), bf16[64,128,128]{2,0,1:T(8,128)(2,1)S(1)}, u32[]{:S(2)}, u32[]{:S(2)}) %all-to-all-start) | async-done | bytes 2097184 | tf_op jit(solution)/shard_map/all_to_all | solution.py:18
  80.8 8.9 %all-to-all-start.2 = ((s32[128,1,8]{2,1,0:T(1,128)}), s32[128,1,8]{2,1,0:T(1,128)S(1)}, u32[]{:S(2)}, u32[]{:S(2)}) async-start(s32[128,1,8]{2,1,0:T(1,128)} %bitcast.25), calls=%async_computation.2 | async-start | bytes 131072 | tf_op jit(solution)/shard_map/all_to_all | solution.py:73
  89.7 1.6 pad_maximum_fusion
  91.2 2.6 gather_fusion.1
  93.9 0.0 copy-start.3
  93.9 5.4 %fusion.10 = f32[64,135,128]{2,0,1:T(8,128)S(1)} fusion(bf16[1,135,128,128]{3,2,1,0:T(8,128)(2,1)} %param.12, bf16[135,64,128]{2,1,0:T(8,128)(2,1)S(1)} %gather_fusion.1), kind=kOutput, calls=%fused_computation.20 | convolution fusion | flops 283115520 | bytes 11059200 | tf_op jit(solution)/shard_map/ctj,tij->cti/dot_general | solution.py:21
  99.3 0.0 copy-done.3
  99.3 4.0 %fusion.34 = f32[64,8,128]{2,1,0:T(8,128)S(1)} fusion(f32[64,135,128]{2,0,1:T(8,128)S(1)} %fusion.10, s32[135]{0:T(256)S(1)} %bitcast.101), kind=kOutput, calls=%fused_computation.31 | convolution fusion | flops 106234936 | bytes 4686364 | tf_op jit(solution)/shard_map/rt,cti->cri/dot_general | solution.py:25
  103.3 0.2 copy.83
  103.5 0.1 fusion.40
  103.6 0.1 copy.76
  103.7 2.2 gather_fusion.2
  105.9 0.0 all-to-all-done.2
  105.9 13.7 %all-to-all-start.1 = ((bf16[64,128,128]{2,0,1:T(8,128)(2,1)}), bf16[64,128,128]{2,0,1:T(8,128)(2,1)S(1)}, u32[]{:S(2)}, u32[]{:S(2)}) async-start(bf16[64,128,128]{2,0,1:T(8,128)(2,1)} %bitcast.13), calls=%async_computation.1 | async-start | bytes 4194304 | tf_op jit(solution)/shard_map/all_to_all | solution.py:18
  119.7 0.1 reshape.190
  119.8 51.1 %all-to-all-done.1 = bf16[64,128,128]{2,0,1:T(8,128)(2,1)S(1)} async-done(((bf16[64,128,128]{2,0,1:T(8,128)(2,1)}), bf16[64,128,128]{2,0,1:T(8,128)(2,1)S(1)}, u32[]{:S(2)}, u32[]{:S(2)}) %all-to-all-start.1) | async-done | bytes 2097184 | tf_op jit(solution)/shard_map/all_to_all | solution.py:18
  170.9 1.6 pad_maximum_fusion.1
  172.5 2.6 gather_fusion.3
  175.1 5.4 %fusion.15 = f32[64,135,128]{2,0,1:T(8,128)S(1)} fusion(bf16[1,135,128,128]{3,2,1,0:T(8,128)(2,1)} %param.12, bf16[135,64,128]{2,1,0:T(8,128)(2,1)S(1)} %gather_fusion.3), kind=kOutput, calls=%fused_computation.21 | convolution fusion | flops 283115520 | bytes 11059200 | tf_op jit(solution)/shard_map/ctj,tij->cti/dot_general | solution.py:21
  180.5 4.0 %fusion.31 = f32[64,8,128]{2,1,0:T(8,128)S(1)} fusion(f32[64,135,128]{2,0,1:T(8,128)S(1)} %fusion.15, s32[135]{0:T(256)S(1)} %bitcast.102), kind=kOutput, calls=%fused_computation.30 | convolution fusion | flops 106234936 | bytes 4686364 | tf_op jit(solution)/shard_map/rt,cti->cri/dot_general | solution.py:25
  184.5 0.2 copy.87
  184.7 0.1 fusion.39
  184.8 0.0 copy-start.4
  184.8 3.2 %gather_fusion.5 = bf16[1024,64]{1,0:T(8,128)(2,1)S(1)} fusion(bf16[64,1024]{0,1:T(8,128)(2,1)S(1)} %fusion.39, s32[1024]{0:T(1024)S(1)} %broadcast_clamp_fusion), kind=kCustom, calls=%fused_computation.5 | custom fusion | bytes 266240 | tf_op jit(solution)/shard_map/gather | solution.py:73
  188.1 0.9 reshape.217
  188.9 8.9 %all-to-all-start.3 = ((bf16[128,2,256]{2,1,0:T(2,128)(2,1)}), bf16[128,2,256]{2,1,0:T(2,128)(2,1)S(1)}, u32[]{:S(2)}, u32[]{:S(2)}) async-start(bf16[128,2,256]{2,1,0:T(2,128)(2,1)} %reshape.217), calls=%async_computation.3 | async-start | bytes 262144 | tf_op jit(solution)/shard_map/all_to_all | solution.py:72
  197.9 0.3 all-reduce.2.cloned.1.call-start
  198.2 0.0 copy-done.4
  198.2 1.3 gather_fusion.4
  199.6 0.0 copy-start.6
  199.6 0.0 copy-start.7
  199.6 11.0 %all-to-all-done.3 = bf16[128,2,256]{2,1,0:T(2,128)(2,1)S(1)} async-done(((bf16[128,2,256]{2,1,0:T(2,128)(2,1)}), bf16[128,2,256]{2,1,0:T(2,128)(2,1)S(1)}, u32[]{:S(2)}, u32[]{:S(2)}) %all-to-all-start.3) | async-done | bytes 131104 | tf_op jit(solution)/shard_map/all_to_all | solution.py:72
  210.6 0.2 reshape.218
  210.8 3.1 %gather_fusion.6 = bf16[512,64]{1,0:T(8,128)(2,1)S(1)} fusion(bf16[64,128,8]{0,2,1:T(8,128)(2,1)S(1)} %bitcast.91, s32[512]{0:T(512)S(1)} %bitcast.89), kind=kCustom, calls=%fused_computation.6 | custom fusion | bytes 135168 | tf_op jit(solution)/shard_map/gather | solution.py:79
  213.9 0.0 copy-done
  213.9 1.5 fusion.24
  215.4 0.0 all-reduce.2.cloned.1.call-update
  215.4 0.8 copy.82
  216.2 46.4 %all-reduce.2.cloned.1.call-done = bf16[1024,512]{0,1:T(8,128)(2,1)} async-done(((bf16[1024,512]{0,1:T(8,128)(2,1)}), bf16[1024,512]{0,1:T(8,128)(2,1)}) %all-reduce.2.cloned.1.call-update) | async-done | bytes 1048592 | tf_op jit(solution)/shard_map/psum | solution.py:85
  262.6 0.0 copy-done.6
  262.6 0.0 copy-done.7
  262.6 3.9 %fusion.20 = f32[1,512]{1,0:T(1,128)} fusion(f32[1024,1]{0,1:T(1,128)S(1)} %bitcast.105, bf16[1024,512]{0,1:T(8,128)(2,1)} %all-reduce.2.cloned.1.call-done, f32[1024]{0:T(1024)S(1)} %copy-done.7), kind=kOutput, calls=%fused_computation.22 | convolution fusion | flops 7864320 | bytes 1058816 | tf_op jit(solution)/shard_map/dot_general | solution.py:87
  (16 shorter events, 0.2 us)
Async XLA Ops:
  7.2 206.7 %copy-start = (bf16[64,1024]{1,0:T(8,128)(2,1)S(1)}, bf16[64,1024]{1,0:T(8,128)(2,1)}, u32[]{:S(2)}) copy-start(bf16[64,1024]{1,0:T(8,128)(2,1)} %param.19) | copy-start | bytes 393220
  11.0 18.6 %copy-start.1 = (bf16[64,1024]{1,0:T(8,128)(2,1)S(1)}, bf16[64,1024]{1,0:T(8,128)(2,1)}, u32[]{:S(2)}) copy-start(bf16[64,1024]{1,0:T(8,128)(2,1)} %param.11) | copy-start | bytes 393220
  11.0 18.8 %copy-start.2 = (s32[512,1]{0,1:T(1,128)S(1)}, s32[512,1]{0,1:T(1,128)}, u32[]{:S(2)}) copy-start(s32[512,1]{0,1:T(1,128)} %param.17) | copy-start | bytes 6148
  11.0 22.8 %copy-start.5 = (s32[1,135]{1,0:T(1,128)S(1)}, s32[1,135]{1,0:T(1,128)}, u32[]{:S(2)}) copy-start(s32[1,135]{1,0:T(1,128)} %param.14) | copy-start | bytes 1624
  11.0 69.8 %all-to-all-start = ((bf16[64,128,128]{2,0,1:T(8,128)(2,1)}), bf16[64,128,128]{2,0,1:T(8,128)(2,1)S(1)}, u32[]{:S(2)}, u32[]{:S(2)}) async-start(bf16[64,128,128]{2,0,1:T(8,128)(2,1)} %bitcast.90), calls=%async_computation | async-start | bytes 4194304 | tf_op jit(solution)/shard_map/all_to_all | solution.py:18
  80.8 25.1 %all-to-all-start.2 = ((s32[128,1,8]{2,1,0:T(1,128)}), s32[128,1,8]{2,1,0:T(1,128)S(1)}, u32[]{:S(2)}, u32[]{:S(2)}) async-start(s32[128,1,8]{2,1,0:T(1,128)} %bitcast.25), calls=%async_computation.2 | async-start | bytes 131072 | tf_op jit(solution)/shard_map/all_to_all | solution.py:73
  93.9 5.4 %copy-start.3 = (s32[1,135]{1,0:T(1,128)S(1)}, s32[1,135]{1,0:T(1,128)}, u32[]{:S(2)}) copy-start(s32[1,135]{1,0:T(1,128)} %param.13) | copy-start | bytes 1624
  105.9 65.0 %all-to-all-start.1 = ((bf16[64,128,128]{2,0,1:T(8,128)(2,1)}), bf16[64,128,128]{2,0,1:T(8,128)(2,1)S(1)}, u32[]{:S(2)}, u32[]{:S(2)}) async-start(bf16[64,128,128]{2,0,1:T(8,128)(2,1)} %bitcast.13), calls=%async_computation.1 | async-start | bytes 4194304 | tf_op jit(solution)/shard_map/all_to_all | solution.py:18
  184.8 13.4 %copy-start.4 = (s32[512]{0:T(512)S(1)}, s32[512]{0:T(512)}, u32[]{:S(2)}) copy-start(s32[512]{0:T(512)} %param.16) | copy-start | bytes 6148
  188.9 21.7 %all-to-all-start.3 = ((bf16[128,2,256]{2,1,0:T(2,128)(2,1)}), bf16[128,2,256]{2,1,0:T(2,128)(2,1)S(1)}, u32[]{:S(2)}, u32[]{:S(2)}) async-start(bf16[128,2,256]{2,1,0:T(2,128)(2,1)} %reshape.217), calls=%async_computation.3 | async-start | bytes 262144 | tf_op jit(solution)/shard_map/all_to_all | solution.py:72
  197.9 64.7 %all-reduce.2.cloned.1.call-start = ((), (), s32[]{:S(2)}) async-start(), calls=%async_computation.4 | async-start | bytes 2097152 | tf_op jit(solution)/shard_map/psum | solution.py:85
  199.6 63.0 %copy-start.6 = (f32[1024]{0:T(1024)S(1)}, f32[1024]{0:T(1024)}, u32[]{:S(2)}) copy-start(f32[1024]{0:T(1024)} %param.21) | copy-start | bytes 12292
  199.6 63.0 %copy-start.7 = (f32[1024]{0:T(1024)S(1)}, f32[1024]{0:T(1024)}, u32[]{:S(2)}) copy-start(f32[1024]{0:T(1024)} %param.20) | copy-start | bytes 12292
Sparse Core Ops, SparseCore 0:
  215.5 47.0 all-reduce.1
where the time goes:
time: 274 us; the launch traced here: 273 us
  waiting for transfers between devices  156 us (57%)
  starting transfers between devices  50.4 us (18%)
  local copies, waits for them, and re-layouts  24.4 us (9%)
  matrix products  24.1 us (9%)
  between operations  14.3 us (5%)
  other arithmetic  4.5 us (2%)
    all_to_all x2, waiting for transfers between devices, propagate(): lax.all_to_all(outgoing, 'node', split_axis=1, concat_axis=1, tiled=True)  98.2 us
    psum x1, waiting for transfers between devices, shards(): lax.psum(partial_value.astype(jnp.bfloat16), 'feat').astype(jnp.float32)  46.4 us
    all_to_all x2, starting transfers between devices, propagate(): lax.all_to_all(outgoing, 'node', split_axis=1, concat_axis=1, tiled=True)  32.3 us
    all_to_all x1, waiting for transfers between devices, shards(): lax.all_to_all(current[:, lax.all_to_all(requests, 'node', split_axis=0,...  11 us
    dot_general x2, matrix products, propagate(): jnp.einsum('ctj,tij->cti', picked, weights, preferred_element_type=jnp.fl...  10.8 us
    all_to_all x1, starting transfers between devices, shards(): lax.all_to_all(current[:, lax.all_to_all(requests, 'node', split_axis=0,...  8.95 us
    all_to_all x1, starting transfers between devices, shards(): lax.all_to_all(requests, 'node', split_axis=0, concat_axis=0, tiled=True)  8.85 us
    dot_general x2, matrix products, propagate(): jnp.einsum('rt,cti->cri', selector, products, precision=lax.Precision.HIG...  7.96 us
  transfers between devices with their start and end apart: 5, of which 4 were waited for; matrix products, arithmetic and copies ran while one was open for 8% of the time, Pallas kernels for 0%

commit v1 on v0

v1 whole, which is shorter than its diff:
```python
import jax
import jax.numpy as jnp
from jax import lax
from jax.experimental import pallas as pl
from jax.experimental.pallas import tpu as pltpu
from jax.sharding import PartitionSpec as P

Z, Y, C, X = 8, 8, 2, 4
RB, B, CAP = 8, 128, 8
HOPS = 2
TELEPORT = 0.1
MESH = pl.DeviceIdType.MESH
F32, BF16, I32 = jnp.float32, jnp.bfloat16, jnp.int32


def dot(left, right, left_dim, right_dim):
    return lax.dot_general(
        left, right, (((left_dim,), (right_dim,)), ((), ())), preferred_element_type=F32
    )


def iota(shape, dim):
    return lax.broadcasted_iota(I32, shape, dim)


def kernel(
    embed, weight_hbm, tile_rows, tile_cols, send_rows, src_local, dst_owner, dst_local, w_in, b_in, w_out,
    out, scores,
    cur0, cur1, cur2, gz0, gy0, gz1, gy1, sa0, sb0, sa1, sb1, ra0, rb0, ra1, rb1,
    weight, total, cols, table, table_s, sr_own, srz, sry, srz_s, sry_s,
    req, reqz, reqm, reqy, pick, pick_src, pick_slot, reply, mid, got,
    wfull, wt, bcol, ocol, had, hadfull,
    local_sem, sz_send, sz_recv, sy_send, sy_recv, a_send, a_recv, b_send, b_recv,
    qz_send, qz_recv, qy_send, qy_recv, pa_send, pa_recv, pb_send, pb_recv,
    rz_send, rz_recv, ry_send, ry_recv, wx_send, wx_recv, hx_send, hx_recv,
):
    parts = Z * Y * C
    yc, zc = Y * C, Z * C
    queries = src_local.shape[1]
    nodes = embed.shape[1]
    half = embed.shape[0] // 2
    me, xf = lax.axis_index("node"), lax.axis_index("feat")
    z, j = me // yc, me % yc
    y, c = j // C, j % C
    k = z * C + c

    def at_a(jd):
        return (z * yc + jd, xf)

    def at_b(kd):
        return (((kd // C) * Y + y) * C + kd % C, xf)

    def at_z(zd):
        return ((zd * Y + y) * C + c, xf)

    def at_y(yd):
        return ((z * Y + yd) * C + c, xf)

    def at_x(xd):
        return (me, xd)

    def push(src, dst, send, recv, device):
        return pltpu.make_async_remote_copy(
            src_ref=src, dst_ref=dst, send_sem=send, recv_sem=recv, device_id=device, device_id_type=MESH
        )

    def each(lo, hi, body):
        def step(i, carry):
            body(i)
            return carry
        lax.fori_loop(lo, hi, step, 0)

    def zigzag(i, n):
        return jnp.where(i % 2 == 1, (i + 1) // 2, n - i // 2)

    barrier = pltpu.get_barrier_semaphore()

    def greet(device):
        pl.semaphore_signal(barrier, inc=1, device_id=device, device_id_type=MESH)

    each(1, yc, lambda e: greet(at_a((j + e) % yc)))
    each(1, zc, lambda e: greet(at_b((k + e) % zc)))
    each(1, X, lambda e: greet(at_x((xf + e) % X)))

    fetch = pltpu.make_async_copy(weight_hbm.at[0], weight, local_sem.at[0])
    fetch.start()
    for r in range(RB):
        for h in range(2):
            cur0[h, r] = embed[h * half:(h + 1) * half, r * B:(r + 1) * B]
    sr_own[...] = send_rows[...].reshape(1, parts)

    pl.semaphore_wait(barrier, yc - 1 + zc - 1 + X - 1)

    def share(hop, cur, gz, gy):
        def go_z(d):
            zd = (z + d) % Z
            push(cur.at[0], gz.at[z], sz_send.at[hop, d], sz_recv.at[hop, z], at_z(zd)).start()
        def go_y(d):
            yd = (y + d) % Y
            push(cur.at[1], gy.at[y], sy_send.at[hop, d], sy_recv.at[hop, y], at_y(yd)).start()
        each(1, Z, lambda i: go_z(zigzag(i, Z)))
        each(1, Y, lambda i: go_y(zigzag(i, Y)))
        gz[z] = cur[0]
        gy[y] = cur[1]

    def shared(hop, cur, gz, gy):
        def end_z(d):
            s = (z + d) % Z
            push(cur.at[0], gz.at[s], sz_send.at[hop, d], sz_recv.at[hop, s], at_z(s)).wait_recv()
        def end_y(d):
            s = (y + d) % Y
            push(cur.at[1], gy.at[s], sy_send.at[hop, d], sy_recv.at[hop, s], at_y(s)).wait_recv()
        each(1, Z, end_z)
        each(1, Y, end_y)

    def deal(hop, gz, gy, sa, sb, ra, rb):
        def fill_a(jd, dst):
            for s in range(Z):
                dst[jd, s] = gz[s, srz_s[s, 0, z * yc + jd]]
        def fill_b(kd, dst):
            for s in range(Y):
                dst[kd, s] = gy[s, sry_s[s, 0, ((kd // C) * Y + y) * C + kd % C]]
        def go_a(i):
            jd = (j + zigzag(i, yc)) % yc
            fill_a(jd, sa)
            push(sa.at[jd], ra.at[j], a_send.at[hop, jd], a_recv.at[hop, j], at_a(jd)).start()
        def go_b(i):
            kd = (k + zigzag(i, zc)) % zc
            fill_b(kd, sb)
            push(sb.at[kd], rb.at[k], b_send.at[hop, kd], b_recv.at[hop, k], at_b(kd)).start()
        each(1, yc, go_a)
        each(1, zc, go_b)
        fill_a(j, ra)
        fill_b(k, rb)

    def dealt(hop, sa, sb, ra, rb):
        def end_a(e):
            s = (j + e) % yc
            push(sa.at[s], ra.at[s], a_send.at[hop, s], a_recv.at[hop, s], at_a(s)).wait_recv()
        def end_b(e):
            s = (k + e) % zc
            push(sb.at[s], rb.at[s], b_send.at[hop, s], b_recv.at[hop, s], at_b(s)).wait_recv()
        each(1, yc, end_a)
        each(1, zc, end_b)

    def combine(cur, ra, rb, nxt):
        def term(s, block):
            product = dot(block, weight[table_s[0, s]], 1, 1)
            total[s] = product + total[table_s[1, s]]
        def column(jd):
            yd, cd = jd // C, jd % C
            for s in range(Z):
                term(jd * Z + s, jnp.concatenate([ra[jd, s], rb[s * C + cd, yd]], axis=0))
        total[parts + RB] = jnp.zeros(total.shape[1:], F32)
        each(0, yc, column)
        for r in range(RB):
            term(parts + r, jnp.concatenate([cur[0, r], cur[1, r]], axis=0))
        for r in range(RB):
            first = jnp.concatenate([cur0[0, r], cur0[1, r]], axis=0).astype(F32)
            new = ((1.0 - TELEPORT) * total[parts + r] + TELEPORT * first).astype(BF16)
            nxt[0, r] = new[:half]
            nxt[1, r] = new[half:]

    share(0, cur0, gz0, gy0)

    def rows_z(d):
        push(sr_own, srz.at[z], rz_send.at[d], rz_recv.at[z], at_z((z + d) % Z)).start()
    def rows_y(d):
        push(sr_own, sry.at[y], ry_send.at[d], ry_recv.at[y], at_y((y + d) % Y)).start()
    each(1, Z, rows_z)
    each(1, Y, rows_y)
    srz[z] = sr_own[...]
    sry[y] = sr_own[...]
    each(1, X, lambda d: push(
        w_in, wfull.at[xf], wx_send.at[d], wx_recv.at[xf], at_x((xf + d) % X)).start())
    wfull[xf] = w_in[...]

    slots = cols.shape[1]
    cols[...] = jnp.full(cols.shape, -1, I32)
    tiles = tile_cols.shape[1]
    cols[0:1, 0:tiles] = tile_cols[...]
    cols[8:9, 0:tiles] = tile_rows[...]
    col = cols[0:1, :]
    peer = col - RB
    peer_slot = (peer % yc) * Z + peer // yc
    slot_of = jnp.where(col < 0, -1, jnp.where(col < RB, parts + col, peer_slot))
    hit = (iota((slots, slots), 0) == slot_of).astype(F32).astype(BF16)
    kind = iota((8, slots), 0)
    facts = jnp.where(kind == 0, iota((8, slots), 1), jnp.where(kind == 1, cols[8:9, :], 1))
    found = dot(facts.astype(F32).astype(BF16), hit, 1, 1)
    row_of = jnp.where(found[2:3, :] > 0.5, found[1:2, :], -1.0)
    row_hit = (iota((128, slots), 0).astype(F32) == row_of).astype(F32).astype(BF16)
    same = dot(row_hit, row_hit, 0, 0)
    before = jnp.where(
        (same > 0.5) & (iota((slots, slots), 0) < iota((slots, slots), 1)), iota((slots, slots), 0).astype(F32), -1.0
    )
    last = jnp.max(before, axis=0, keepdims=True)
    table[0:1, :] = jnp.clip(found[0:1, :].astype(I32), 0, tiles - 1)
    table[1:2, :] = jnp.clip(jnp.where(last < 0.0, float(parts + RB), last).astype(I32), 0, parts + RB)
    to_smem = pltpu.make_async_copy(table, table_s, local_sem.at[1])
    to_smem.start()

    owner = dst_owner[...]
    owns = (iota((parts, queries), 0) == owner).astype(F32).astype(BF16)
    alike = dot(owns, owns, 0, 0)
    earlier = iota((queries, queries), 0) < iota((queries, queries), 1)
    rank = jnp.sum(jnp.where(earlier, alike, 0.0), axis=0, keepdims=True).astype(I32)
    place = iota((128, queries), 0) == rank
    high, low = dst_local[...] // 32, dst_local[...] % 32
    ask_high = dot(owns, jnp.where(place, high, 0).astype(F32).astype(BF16), 1, 1)
    ask_low = dot(owns, jnp.where(place, low, 0).astype(F32).astype(BF16), 1, 1)
    req[...] = (ask_high * 32.0 + ask_low).astype(I32).reshape(Z, yc, 128)
    def ask_z(d):
        zd = (z + d) % Z
        push(req.at[zd], reqz.at[z], qz_send.at[d], qz_recv.at[z], at_z(zd)).start()
    each(1, Z, ask_z)
    reqz[z] = req[z]
    slot = owner * CAP + rank
    pick_slot[...] = (iota(pick_slot.shape, 0) == slot).astype(F32).astype(BF16)
    pick_src[...] = (iota(pick_src.shape, 0) == src_local[...]).astype(F32).astype(BF16)

    def rows_z_end(d):
        s = (z + d) % Z
        push(sr_own, srz.at[s], rz_send.at[d], rz_recv.at[s], at_z(s)).wait_recv()
    def rows_y_end(d):
        s = (y + d) % Y
        push(sr_own, sry.at[s], ry_send.at[d], ry_recv.at[s], at_y(s)).wait_recv()
    each(1, Z, rows_z_end)
    each(1, Y, rows_y_end)
    rows_copies = [
        pltpu.make_async_copy(srz, srz_s, local_sem.at[2]),
        pltpu.make_async_copy(sry, sry_s, local_sem.at[3]),
    ]
    for copy in rows_copies:
        copy.start()
    for copy in rows_copies:
        copy.wait()
    shared(0, cur0, gz0, gy0)
    deal(0, gz0, gy0, sa0, sb0, ra0, rb0)

    def ask_z_end(d):
        s = (z + d) % Z
        push(req.at[s], reqz.at[s], qz_send.at[d], qz_recv.at[s], at_z(s)).wait_recv()
    each(1, Z, ask_z_end)
    for jd in range(yc):
        reqm[jd] = jnp.concatenate([reqz[s, jd:jd + 1, :] for s in range(Z)], axis=0)
    def ask_y(e):
        jd = (j + e) % yc
        push(reqm.at[jd], reqy.at[j], qy_send.at[e], qy_recv.at[j], at_a(jd)).start()
    each(1, yc, ask_y)
    reqy[j] = reqm[j]

    def w_end(d):
        s = (xf + d) % X
        push(w_in, wfull.at[s], wx_send.at[d], wx_recv.at[s], at_x(s)).wait_recv()
    each(1, X, w_end)
    hidden_units = w_in.shape[1]
    channels = w_in.shape[0]
    for n in range(hidden_units // 128):
        lanes = slice(n * 128, (n + 1) * 128)
        whole = jnp.concatenate([wfull[s, :, lanes] for s in range(X)], axis=0)
        wt[lanes, :] = whole.astype(F32).T.astype(BF16)
        bcol[lanes, :] = jnp.broadcast_to(b_in[0:1, lanes], (128, 128)).T
        ocol[lanes, :] = jnp.broadcast_to(w_out[0:1, lanes], (128, 128)).T

    to_smem.wait()
    fetch.wait()
    dealt(0, sa0, sb0, ra0, rb0)
    combine(cur0, ra0, rb0, cur1)

    share(1, cur1, gz1, gy1)
    shared(1, cur1, gz1, gy1)
    deal(1, gz1, gy1, sa1, sb1, ra1, rb1)

    def ask_y_end(e):
        s = (j + e) % yc
        push(reqm.at[s], reqy.at[s], qy_send.at[e], qy_recv.at[s], at_a(s)).wait_recv()
    each(1, yc, ask_y_end)
    asked = reqy[...].reshape(yc * Z, 128)
    for n in range(CAP):
        pick[n] = (iota((parts, nodes), 1) == asked[:, n:n + 1]).astype(F32).astype(BF16)

    dealt(1, sa1, sb1, ra1, rb1)
    combine(cur1, ra1, rb1, cur2)
    for r in range(RB):
        for h in range(2):
            out[h * half:(h + 1) * half, r * B:(r + 1) * B] = cur2[h, r]

    final = out[...]
    def reply_rows(n):
        rows = dot(pick[n], final, 1, 1)
        return rows.reshape(yc, Z, 1, channels)
    reply[...] = jnp.concatenate([reply_rows(n) for n in range(CAP)], axis=2).astype(BF16)
    def reply_a(i):
        jd = (j + i) % yc
        push(reply.at[jd], mid.at[j], pa_send.at[i], pa_recv.at[j], at_a(jd)).start()
    each(1, yc, reply_a)
    mid[j] = reply[j]
    source = dot(final, pick_src[...], 1, 0)
    def reply_a_end(e):
        s = (j + e) % yc
        push(reply.at[s], mid.at[s], pa_send.at[e], pa_recv.at[s], at_a(s)).wait_recv()
    each(1, yc, reply_a_end)
    def reply_z(d):
        zd = (z + d) % Z
        push(mid.at[:, zd], got.at[z], pb_send.at[d], pb_recv.at[z], at_z(zd)).start()
    each(1, Z, reply_z)
    got[z] = mid[:, z]
    def reply_z_end(d):
        s = (z + d) % Z
        push(mid.at[:, s], got.at[s], pb_send.at[d], pb_recv.at[s], at_z(s)).wait_recv()
    each(1, Z, reply_z_end)
    target = dot(got[...].reshape(parts * CAP, channels), pick_slot[...], 0, 0)
    had[...] = (source * target).astype(BF16)
    def had_x(d):
        push(had, hadfull.at[xf], hx_send.at[d], hx_recv.at[xf], at_x((xf + d) % X)).start()
    each(1, X, had_x)
    hadfull[xf] = had[...]
    def had_x_end(d):
        s = (xf + d) % X
        push(had, hadfull.at[s], hx_send.at[d], hx_recv.at[s], at_x(s)).wait_recv()
    each(1, X, had_x_end)
    everything = hadfull[...].reshape(X * channels, queries)
    score = jnp.zeros((8, queries), F32)
    for n in range(hidden_units // 128):
        lanes = slice(n * 128, (n + 1) * 128)
        hidden = dot(wt[lanes, :], everything, 1, 0)
        bias, gain = bcol[lanes, :], ocol[lanes, :]
        if queries > 128:
            bias, gain = (jnp.concatenate([v] * (queries // 128), axis=1) for v in (bias, gain))
        else:
            bias, gain = bias[:, :queries], gain[:, :queries]
        active = jnp.maximum(hidden + bias, 0.0) * gain
        score = score + jnp.sum(active.reshape(16, 8, queries), axis=0)
    scores[...] = jnp.sum(score, axis=0, keepdims=True)

    for hop, cur, gz, gy, sa, sb, ra, rb in (
        (0, cur0, gz0, gy0, sa0, sb0, ra0, rb0), (1, cur1, gz1, gy1, sa1, sb1, ra1, rb1)
    ):
        each(1, Z, lambda d: push(
            cur.at[0], gz.at[z], sz_send.at[hop, d], sz_recv.at[hop, z], at_z((z + d) % Z)).wait_send())
        each(1, Y, lambda d: push(
            cur.at[1], gy.at[y], sy_send.at[hop, d], sy_recv.at[hop, y], at_y((y + d) % Y)).wait_send())
        def left_a(e):
            jd = (j + e) % yc
            push(sa.at[jd], ra.at[j], a_send.at[hop, jd], a_recv.at[hop, j], at_a(jd)).wait_send()
        def left_b(e):
            kd = (k + e) % zc
            push(sb.at[kd], rb.at[k], b_send.at[hop, kd], b_recv.at[hop, k], at_b(kd)).wait_send()
        each(1, yc, left_a)
        each(1, zc, left_b)
    def left_z(d):
        zd = (z + d) % Z
        push(sr_own, srz.at[z], rz_send.at[d], rz_recv.at[z], at_z(zd)).wait_send()
        push(req.at[zd], reqz.at[z], qz_send.at[d], qz_recv.at[z], at_z(zd)).wait_send()
        push(mid.at[:, zd], got.at[z], pb_send.at[d], pb_recv.at[z], at_z(zd)).wait_send()
    each(1, Z, left_z)
    each(1, Y, lambda d: push(
        sr_own, sry.at[y], ry_send.at[d], ry_recv.at[y], at_y((y + d) % Y)).wait_send())
    def left_y(e):
        jd = (j + e) % yc
        push(reqm.at[jd], reqy.at[j], qy_send.at[e], qy_recv.at[j], at_a(jd)).wait_send()
        push(reply.at[jd], mid.at[j], pa_send.at[e], pa_recv.at[j], at_a(jd)).wait_send()
    each(1, yc, left_y)
    def left_x(d):
        xd = (xf + d) % X
        push(w_in, wfull.at[xf], wx_send.at[d], wx_recv.at[xf], at_x(xd)).wait_send()
        push(had, hadfull.at[xf], hx_send.at[d], hx_recv.at[xf], at_x(xd)).wait_send()
    each(1, X, left_x)


def shards(
    embed, tile_weight, tile_rows, tile_cols, send_rows, src_local, dst_owner, dst_local, w_in, b_in, w_out
):
    parts, yc, zc = Z * Y * C, Y * C, Z * C
    channels, nodes = embed.shape
    half = channels // 2
    queries, hidden = src_local.shape[0], w_in.shape[1]
    tiles = tile_rows.shape[1]
    slots = 256
    V, S, D = pltpu.VMEM, pltpu.SMEM, pltpu.SemaphoreType.DMA
    cur = [V((2, RB, half, B), BF16)] * 3
    near = [V((n, RB, half, B), BF16) for n in (Z, Y, Z, Y)]
    deal = [V((n, m, half, B), BF16) for n, m in ((yc, Z), (zc, Y))]
    scratch = cur + near + deal * 4 + [
        V((tiles, B, B), BF16), V((parts + RB + 1, channels, B), F32),
        V((16, slots), I32), V((8, slots), I32), S((8, slots), I32),
        V((1, parts), I32), V((Z, 1, parts), I32), V((Y, 1, parts), I32), S((Z, 1, parts), I32), S((Y, 1, parts), I32),
        V((Z, yc, 128), I32), V((Z, yc, 128), I32), V((yc, Z, 128), I32), V((yc, Z, 128), I32),
        V((CAP, parts, nodes), BF16), V((nodes, queries), BF16), V((parts * CAP, queries), BF16),
        V((yc, Z, CAP, channels), BF16), V((yc, Z, CAP, channels), BF16), V((Z, yc, CAP, channels), BF16),
        V((X, channels, hidden), BF16), V((hidden, X * channels), BF16), V((hidden, 128), F32), V((hidden, 128), F32),
        V((channels, queries), BF16), V((X, channels, queries), BF16),
        D((4,)), D((HOPS, Z)), D((HOPS, Z)), D((HOPS, Y)), D((HOPS, Y)),
        D((HOPS, yc)), D((HOPS, yc)), D((HOPS, zc)), D((HOPS, zc)),
        D((Z,)), D((Z,)), D((yc,)), D((yc,)), D((yc,)), D((yc,)), D((Z,)), D((Z,)),
        D((Z,)), D((Z,)), D((Y,)), D((Y,)), D((X,)), D((X,)), D((X,)), D((X,)),
    ]
    vmem = pl.BlockSpec(memory_space=pltpu.VMEM)
    propagated, scores = pl.pallas_call(
        kernel,
        out_shape=(
            jax.ShapeDtypeStruct((channels, nodes), BF16),
            jax.ShapeDtypeStruct((1, queries), F32),
        ),
        in_specs=[vmem, pl.BlockSpec(memory_space=pl.ANY)] + [vmem] * 9,
        out_specs=(vmem, vmem),
        scratch_shapes=scratch,
        compiler_params=pltpu.CompilerParams(
            collective_id=0, has_side_effects=True, vmem_limit_bytes=56 * 1024 * 1024
        ),
    )(
        embed, tile_weight, tile_rows, tile_cols, send_rows,
        src_local.reshape(1, queries), dst_owner.reshape(1, queries), dst_local.reshape(1, queries),
        w_in, b_in.reshape(1, hidden), w_out.reshape(1, hidden),
    )
    return propagated, scores.reshape(queries)


def solution(mesh):
    placed = (
        P("feat", "node"),
        P("node", None, None, None),
        P("node", None),
        P("node", None),
        P("node", None),
        P("node"),
        P("node", None),
        P("node"),
        P("feat", None),
        P(),
        P(),
    )
    return jax.shard_map(
        shards,
        mesh=mesh,
        in_specs=placed,
        out_specs=(P("feat", "node"), P("node")),
        check_vma=False,
    )
```

time: 274 us -> 142 us (0.52)
  waiting for transfers between devices: 156 us -> 0 us
  Pallas kernels: 0 us -> 138 us
  starting transfers between devices: 50.4 us -> 0 us
  matrix products: 24.1 us -> 0 us
  local copies, waits for them, and re-layouts: 24.4 us -> 2.83 us
  between operations: 14.3 us -> 0.64 us
  other arithmetic: 4.5 us -> 0 us
    pallas_call x0 -> x1, Pallas kernels: none -> 138 us  [shards(): pl.pallas_call(kernel, out_shape=(jax.ShapeDtypeStruct((channels, nodes),...]
    all_to_all x4 -> x0, waiting for transfers between devices: 109 us -> none  [the longest x2 98.2 us: propagate(): lax.all_to_all(outgoing, 'node', split_axis=1, concat_axis=1, tiled=True)]
    all_to_all x4 -> x0, starting transfers between devices: 50.1 us -> none  [the longest x2 32.3 us: propagate(): lax.all_to_all(outgoing, 'node', split_axis=1, concat_axis=1, tiled=True)]
    psum x1 -> x0, waiting for transfers between devices: 46.4 us -> none  [shards(): lax.psum(partial_value.astype(jnp.bfloat16), 'feat').astype(jnp.float32)]
    dot_general x6 -> x0, matrix products: 24.1 us -> none  [the longest x2 10.8 us: propagate(): jnp.einsum('ctj,tij->cti', picked, weights, preferred_element_type=jnp.fl...]
    gather x7 -> x0, local copies, waits for them, and re-layouts: 17.1 us -> none  [the longest x2 5.21 us: propagate(): picked = sources[:, tile_col, :]]
    concatenate x3 -> x0, other arithmetic: 3.15 us -> none  [the longest x2 3.13 us: propagate(): sources = jnp.concatenate([blocked, incoming], axis=1)]
  transfers between devices with their start and end apart: 5 -> 0, of which waited for: 4 -> 0; matrix products, arithmetic and copies ran while one was open for 8% -> 0% of each run, Pallas kernels for 0% -> 0%
where the time goes in v1:
time: 142 us
  Pallas kernels  138 us (97%)
  local copies, waits for them, and re-layouts  2.83 us (2%)
    pallas_call x1, Pallas kernels, shards(): pl.pallas_call(kernel, out_shape=(jax.ShapeDtypeStruct((channels, nodes),...  138 us

profile of v1, /device:TPU:1, one launch (start us, length us, event | category | flops | bytes accessed | tf_op | source)
XLA Modules:
  0.0 141.8 jit_solution(5921215873110327878)
XLA Ops:
  0.6 138.3 %shard_map.122 = (bf16[64,1024]{1,0:T(8,128)(2,1)}, f32[1,512]{1,0:T(1,128)}) custom-call(bf16[64,1024]{1,0:T(8,128)(2,1)} %embed.1, bf16[1,135,128,128]{3,2,1,0:T(8,128)(2,1)} %weight_hbm.1, s32[1,135]{1,0:T(1,128)} %tile_rows.1, s32[1,135]{1,0:T(1,128)} %tile_cols.1, s32[1,128]{1,0:T(1,128)} %send_rows.1, s32[1,512]{1,0:T(1,128)} %bitcast.8, ...), custom_call_target="tpu_custom_call" | custom-call | tf_op jit(solution)/shard_map/pallas_call | solution.py:400
  139.0 1.6 %copy.15 = bf16[64,1024]{1,0:T(8,128)(2,1)} copy(bf16[64,1024]{1,0:T(8,128)(2,1)} %get-tuple-element.8) | data formatting | bytes 262144
  140.5 1.3 copy.16

commit v2 on v1

--- a/solution.py
+++ b/solution.py
@@ -91,27 +91,51 @@
 
     pl.semaphore_wait(barrier, yc - 1 + zc - 1 + X - 1)
 
+    def ring_copies(hop, gz, gy, step, piece, way):
+        rows = pl.ds(piece * (RB // 2), RB // 2)
+        sz, sy = (z - way * step) % Z, (y - way * step) % Y
+        side = 0 if way == 1 else 1
+        return (
+            push(gz.at[sz, rows], gz.at[sz, rows], sz_send.at[hop, side, step, piece],
+                 sz_recv.at[hop, side, step, piece], at_z((z + way) % Z)),
+            push(gy.at[sy, rows], gy.at[sy, rows], sy_send.at[hop, side, step, piece],
+                 sy_recv.at[hop, side, step, piece], at_y((y + way) % Y)),
+        )
+
+    ring = [
+        (step, piece, way)
+        for step in range(Z // 2) for piece in range(2) for way in (1, -1)
+        if step < Z // 2 - 1 or piece == (0 if way == 1 else 1)
+    ]
+
+    def arrived(hop, gz, gy, step, piece, way):
+        rows = pl.ds(piece * (RB // 2), RB // 2)
+        sz, sy = (z - way * (step + 1)) % Z, (y - way * (step + 1)) % Y
+        side = 0 if way == 1 else 1
+        push(gz.at[sz, rows], gz.at[sz, rows], sz_send.at[hop, side, step, piece],
+             sz_recv.at[hop, side, step, piece], at_z((z + way) % Z)).wait_recv()
+        push(gy.at[sy, rows], gy.at[sy, rows], sy_send.at[hop, side, step, piece],
+             sy_recv.at[hop, side, step, piece], at_y((y + way) % Y)).wait_recv()
+
     def share(hop, cur, gz, gy):
-        def go_z(d):
-            zd = (z + d) % Z
-            push(cur.at[0], gz.at[z], sz_send.at[hop, d], sz_recv.at[hop, z], at_z(zd)).start()
-        def go_y(d):
-            yd = (y + d) % Y
-            push(cur.at[1], gy.at[y], sy_send.at[hop, d], sy_recv.at[hop, y], at_y(yd)).start()
-        each(1, Z, lambda i: go_z(zigzag(i, Z)))
-        each(1, Y, lambda i: go_y(zigzag(i, Y)))
         gz[z] = cur[0]
         gy[y] = cur[1]
-
-    def shared(hop, cur, gz, gy):
-        def end_z(d):
-            s = (z + d) % Z
-            push(cur.at[0], gz.at[s], sz_send.at[hop, d], sz_recv.at[hop, s], at_z(s)).wait_recv()
-        def end_y(d):
-            s = (y + d) % Y
-            push(cur.at[1], gy.at[s], sy_send.at[hop, d], sy_recv.at[hop, s], at_y(s)).wait_recv()
-        each(1, Z, end_z)
-        each(1, Y, end_y)
+        for step, piece, way in ring:
+            if step == 0:
+                for copy in ring_copies(hop, gz, gy, step, piece, way):
+                    copy.start()
+
+    def shared(hop, gz, gy):
+        passed = set()
+        for step, piece, way in ring:
+            if step > 0:
+                arrived(hop, gz, gy, step - 1, piece, way)
+                passed.add((step - 1, piece, way))
+                for copy in ring_copies(hop, gz, gy, step, piece, way):
+                    copy.start()
+        for one in ring:
+            if one not in passed:
+                arrived(hop, gz, gy, *one)
 
     def deal(hop, gz, gy, sa, sb, ra, rb):
         def fill_a(jd, dst):
@@ -120,39 +144,53 @@
         def fill_b(kd, dst):
             for s in range(Y):
                 dst[kd, s] = gy[s, sry_s[s, 0, ((kd // C) * Y + y) * C + kd % C]]
-        def go_a(i):
-            jd = (j + zigzag(i, yc)) % yc
+        def go_a(jd):
             fill_a(jd, sa)
             push(sa.at[jd], ra.at[j], a_send.at[hop, jd], a_recv.at[hop, j], at_a(jd)).start()
-        def go_b(i):
-            kd = (k + zigzag(i, zc)) % zc
+        def go_b(kd):
             fill_b(kd, sb)
             push(sb.at[kd], rb.at[k], b_send.at[hop, kd], b_recv.at[hop, k], at_b(kd)).start()
-        each(1, yc, go_a)
-        each(1, zc, go_b)
         fill_a(j, ra)
         fill_b(k, rb)
-
-    def dealt(hop, sa, sb, ra, rb):
-        def end_a(e):
-            s = (j + e) % yc
+        def ring_step(i):
+            if C == 2:
+                @pl.when(i == 0)
+                def _():
+                    go_a(y * C + 1 - c)
+                    go_b(z * C + 1 - c)
+            @pl.when(i > 0)
+            def _():
+                yd, zd = (y + zigzag(i, Y)) % Y, (z + zigzag(i, Z)) % Z
+                for cd in range(C):
+                    go_a(yd * C + cd)
+                    go_b(zd * C + cd)
+        each(0, Y, ring_step)
+
+    def combine(hop, cur, sa, sb, ra, rb, nxt):
+        def end_a(s):
             push(sa.at[s], ra.at[s], a_send.at[hop, s], a_recv.at[hop, s], at_a(s)).wait_recv()
-        def end_b(e):
-            s = (k + e) % zc
+        def end_b(s):
             push(sb.at[s], rb.at[s], b_send.at[hop, s], b_recv.at[hop, s], at_b(s)).wait_recv()
-        each(1, yc, end_a)
-        each(1, zc, end_b)
-
-    def combine(cur, ra, rb, nxt):
         def term(s, block):
             product = dot(block, weight[table_s[0, s]], 1, 1)
             total[s] = product + total[table_s[1, s]]
-        def column(jd):
-            yd, cd = jd // C, jd % C
-            for s in range(Z):
-                term(jd * Z + s, jnp.concatenate([ra[jd, s], rb[s * C + cd, yd]], axis=0))
+        def pair(s, zi, yi):
+            zs, ys = (z + Z - zigzag(zi, Z)) % Z, (y + Y - zigzag(yi, Y)) % Y
+            for cs in range(C):
+                term(s * C + cs, jnp.concatenate([ra[ys * C + cs, zs], rb[zs * C + cs, ys]], axis=0))
         total[parts + RB] = jnp.zeros(total.shape[1:], F32)
-        each(0, yc, column)
+        for n in range(Z):
+            zs, ys = (z + Z - zigzag(n, Z)) % Z, (y + Y - zigzag(n, Y)) % Y
+            if n > 0:
+                for cs in range(C):
+                    end_a(ys * C + cs)
+                    end_b(zs * C + cs)
+            elif C == 2:
+                end_a(y * C + 1 - c)
+                end_b(z * C + 1 - c)
+            each(0, n + 1, lambda m: pair(n * n + m, n, m))
+            if n > 0:
+                each(0, n, lambda m: pair(n * n + n + 1 + m, m, n))
         for r in range(RB):
             term(parts + r, jnp.concatenate([cur[0, r], cur[1, r]], axis=0))
         for r in range(RB):
@@ -182,7 +220,11 @@
     cols[8:9, 0:tiles] = tile_rows[...]
     col = cols[0:1, :]
     peer = col - RB
-    peer_slot = (peer % yc) * Z + peer // yc
+    def ring_place(far, n):
+        return jnp.where(far == 0, 0, jnp.where(far <= n // 2, 2 * far - 1, 2 * (n - far)))
+    zi = ring_place((z + Z - peer // yc) % Z, Z)
+    yi = ring_place((y + Y - peer % yc // C) % Y, Y)
+    peer_slot = jnp.where(zi >= yi, zi * zi + yi, yi * yi + yi + 1 + zi) * C + peer % C
     slot_of = jnp.where(col < 0, -1, jnp.where(col < RB, parts + col, peer_slot))
     hit = (iota((slots, slots), 0) == slot_of).astype(F32).astype(BF16)
     kind = iota((8, slots), 0)
@@ -215,8 +257,11 @@
         push(req.at[zd], reqz.at[z], qz_send.at[d], qz_recv.at[z], at_z(zd)).start()
     each(1, Z, ask_z)
     reqz[z] = req[z]
-    slot = owner * CAP + rank
-    pick_slot[...] = (iota(pick_slot.shape, 0) == slot).astype(F32).astype(BF16)
+    fold = CAP // 2
+    spot = owner * fold + rank % fold
+    for side in range(2):
+        spot_side = jnp.where(rank // fold == side, spot, -1)
+        pick_slot[side] = (iota(pick_slot.shape[1:], 0) == spot_side).astype(F32).astype(BF16)
     pick_src[...] = (iota(pick_src.shape, 0) == src_local[...]).astype(F32).astype(BF16)
 
     def rows_z_end(d):
@@ -235,7 +280,7 @@
         copy.start()
     for copy in rows_copies:
         copy.wait()
-    shared(0, cur0, gz0, gy0)
+    shared(0, gz0, gy0)
     deal(0, gz0, gy0, sa0, sb0, ra0, rb0)
 
     def ask_z_end(d):
@@ -265,32 +310,34 @@
 
     to_smem.wait()
     fetch.wait()
-    dealt(0, sa0, sb0, ra0, rb0)
-    combine(cur0, ra0, rb0, cur1)
+    combine(0, cur0, sa0, sb0, ra0, rb0, cur1)
 
     share(1, cur1, gz1, gy1)
-    shared(1, cur1, gz1, gy1)
+    shared(1, gz1, gy1)
     deal(1, gz1, gy1, sa1, sb1, ra1, rb1)
 
     def ask_y_end(e):
         s = (j + e) % yc
         push(reqm.at[s], reqy.at[s], qy_send.at[e], qy_recv.at[s], at_a(s)).wait_recv()
     each(1, yc, ask_y_end)
-    asked = reqy[...].reshape(yc * Z, 128)
-    for n in range(CAP):
-        pick[n] = (iota((parts, nodes), 1) == asked[:, n:n + 1]).astype(F32).astype(BF16)
-
-    dealt(1, sa1, sb1, ra1, rb1)
-    combine(cur1, ra1, rb1, cur2)
+    asked = reqy[...].reshape(parts, 128).astype(F32)
+    spread = (iota((parts * fold, parts), 0) // fold == iota((parts * fold, parts), 1)).astype(F32)
+    wide = lax.dot_general(
+        spread, asked, (((1,), (0,)), ((), ())), precision=lax.Precision.HIGHEST, preferred_element_type=F32
+    )
+    for side in range(2):
+        mine = iota(wide.shape, 1) == iota(wide.shape, 0) % fold + side * fold
+        node = jnp.sum(jnp.where(mine, wide, 0.0), axis=1, keepdims=True).astype(I32)
+        pick[side] = (iota((parts * fold, nodes), 1) == node).astype(F32).astype(BF16)
+
+    combine(1, cur1, sa1, sb1, ra1, rb1, cur2)
     for r in range(RB):
         for h in range(2):
             out[h * half:(h + 1) * half, r * B:(r + 1) * B] = cur2[h, r]
 
     final = out[...]
-    def reply_rows(n):
-        rows = dot(pick[n], final, 1, 1)
-        return rows.reshape(yc, Z, 1, channels)
-    reply[...] = jnp.concatenate([reply_rows(n) for n in range(CAP)], axis=2).astype(BF16)
+    rows = jnp.concatenate([dot(pick[side], final, 1, 1) for side in range(2)], axis=1)
+    reply[...] = rows.reshape(yc, Z, fold, 2 * channels).astype(BF16)
     def reply_a(i):
         jd = (j + i) % yc
         push(reply.at[jd], mid.at[j], pa_send.at[i], pa_recv.at[j], at_a(jd)).start()
@@ -310,7 +357,8 @@
         s = (z + d) % Z
         push(mid.at[:, s], got.at[s], pb_send.at[d], pb_recv.at[s], at_z(s)).wait_recv()
     each(1, Z, reply_z_end)
-    target = dot(got[...].reshape(parts * CAP, channels), pick_slot[...], 0, 0)
+    replies = got[...].reshape(parts * fold, 2 * channels)
+    target = dot(replies, pick_slot[0], 0, 0)[:channels] + dot(replies, pick_slot[1], 0, 0)[channels:]
     had[...] = (source * target).astype(BF16)
     def had_x(d):
         push(had, hadfull.at[xf], hx_send.at[d], hx_recv.at[xf], at_x((xf + d) % X)).start()
@@ -334,13 +382,12 @@
         score = score + jnp.sum(active.reshape(16, 8, queries), axis=0)
     scores[...] = jnp.sum(score, axis=0, keepdims=True)
 
-    for hop, cur, gz, gy, sa, sb, ra, rb in (
-        (0, cur0, gz0, gy0, sa0, sb0, ra0, rb0), (1, cur1, gz1, gy1, sa1, sb1, ra1, rb1)
+    for hop, gz, gy, sa, sb, ra, rb in (
+        (0, gz0, gy0, sa0, sb0, ra0, rb0), (1, gz1, gy1, sa1, sb1, ra1, rb1)
     ):
-        each(1, Z, lambda d: push(
-            cur.at[0], gz.at[z], sz_send.at[hop, d], sz_recv.at[hop, z], at_z((z + d) % Z)).wait_send())
-        each(1, Y, lambda d: push(
-            cur.at[1], gy.at[y], sy_send.at[hop, d], sy_recv.at[hop, y], at_y((y + d) % Y)).wait_send())
+        for one in ring:
+            for copy in ring_copies(hop, gz, gy, *one):
+                copy.wait_send()
         def left_a(e):
             jd = (j + e) % yc
             push(sa.at[jd], ra.at[j], a_send.at[hop, jd], a_recv.at[hop, j], at_a(jd)).wait_send()
@@ -377,7 +424,7 @@
     half = channels // 2
     queries, hidden = src_local.shape[0], w_in.shape[1]
     tiles = tile_rows.shape[1]
-    slots = 256
+    slots, fold = 256, CAP // 2
     V, S, D = pltpu.VMEM, pltpu.SMEM, pltpu.SemaphoreType.DMA
     cur = [V((2, RB, half, B), BF16)] * 3
     near = [V((n, RB, half, B), BF16) for n in (Z, Y, Z, Y)]
@@ -387,11 +434,11 @@
         V((16, slots), I32), V((8, slots), I32), S((8, slots), I32),
         V((1, parts), I32), V((Z, 1, parts), I32), V((Y, 1, parts), I32), S((Z, 1, parts), I32), S((Y, 1, parts), I32),
         V((Z, yc, 128), I32), V((Z, yc, 128), I32), V((yc, Z, 128), I32), V((yc, Z, 128), I32),
-        V((CAP, parts, nodes), BF16), V((nodes, queries), BF16), V((parts * CAP, queries), BF16),
-        V((yc, Z, CAP, channels), BF16), V((yc, Z, CAP, channels), BF16), V((Z, yc, CAP, channels), BF16),
+        V((2, parts * fold, nodes), BF16), V((nodes, queries), BF16), V((2, parts * fold, queries), BF16),
+        V((yc, Z, fold, 2 * channels), BF16), V((yc, Z, fold, 2 * channels), BF16), V((Z, yc, fold, 2 * channels), BF16),
         V((X, channels, hidden), BF16), V((hidden, X * channels), BF16), V((hidden, 128), F32), V((hidden, 128), F32),
         V((channels, queries), BF16), V((X, channels, queries), BF16),
-        D((4,)), D((HOPS, Z)), D((HOPS, Z)), D((HOPS, Y)), D((HOPS, Y)),
+        D((4,)), D((HOPS, 2, Z // 2, 2)), D((HOPS, 2, Z // 2, 2)), D((HOPS, 2, Y // 2, 2)), D((HOPS, 2, Y // 2, 2)),
         D((HOPS, yc)), D((HOPS, yc)), D((HOPS, zc)), D((HOPS, zc)),
         D((Z,)), D((Z,)), D((yc,)), D((yc,)), D((yc,)), D((yc,)), D((Z,)), D((Z,)),
         D((Z,)), D((Z,)), D((Y,)), D((Y,)), D((X,)), D((X,)), D((X,)), D((X,)),

time: 142 us -> 134 us (0.944)
  Pallas kernels: 138 us -> 130 us
    pallas_call x1, Pallas kernels: 138 us -> 130 us  [shards(): pl.pallas_call(kernel, out_shape=(jax.ShapeDtypeStruct((channels, nodes),...]
where the time goes in v2:
time: 134 us; the launch traced here: 133 us
  Pallas kernels  130 us (97%)
  local copies, waits for them, and re-layouts  2.83 us (2%)
    pallas_call x1, Pallas kernels, shards(): pl.pallas_call(kernel, out_shape=(jax.ShapeDtypeStruct((channels, nodes),...  130 us
    unnamed x2, local copies, waits for them, and re-layouts  2.83 us

profile of v2, /device:TPU:1, one launch (start us, length us, event | category | flops | bytes accessed | tf_op | source)
XLA Modules:
  0.0 133.5 jit_solution(2024257623134006096)
XLA Ops:
  0.6 130.0 %shard_map.122 = (bf16[64,1024]{1,0:T(8,128)(2,1)}, f32[1,512]{1,0:T(1,128)}) custom-call(bf16[64,1024]{1,0:T(8,128)(2,1)} %embed.1, bf16[1,135,128,128]{3,2,1,0:T(8,128)(2,1)} %weight_hbm.1, s32[1,135]{1,0:T(1,128)} %tile_rows.1, s32[1,135]{1,0:T(1,128)} %tile_cols.1, s32[1,128]{1,0:T(1,128)} %send_rows.1, s32[1,512]{1,0:T(1,128)} %bitcast.8, ...), custom_call_target="tpu_custom_call" | custom-call | tf_op jit(solution)/shard_map/pallas_call | solution.py:447
  130.7 1.6 %copy.15 = bf16[64,1024]{1,0:T(8,128)(2,1)} copy(bf16[64,1024]{1,0:T(8,128)(2,1)} %get-tuple-element.8) | data formatting | bytes 262144
  132.2 1.3 copy.16

commit v3 on v2

--- a/solution.py
+++ b/solution.py
@@ -24,10 +24,11 @@
 
 
 def kernel(
-    embed, weight_hbm, tile_rows, tile_cols, send_rows, src_local, dst_owner, dst_local, w_in, b_in, w_out,
-    out, scores,
+    embed_in, weight_hbm, tile_rows_in, tile_cols_in, send_rows_in, src_local_in, dst_owner_in, dst_local_in,
+    w_in_in, b_in_in, w_out_in, out, scores,
+    embed, tile_rows, tile_cols, sr_own, src_local, dst_owner, dst_local, w_in, b_in, w_out,
     cur0, cur1, cur2, gz0, gy0, gz1, gy1, sa0, sb0, sa1, sb1, ra0, rb0, ra1, rb1,
-    weight, total, cols, table, table_s, sr_own, srz, sry, srz_s, sry_s,
+    weight, total, own, cols, table, table_s, srz, sry, srz_s, sry_s,
     req, reqz, reqm, reqy, pick, pick_src, pick_slot, reply, mid, got,
     wfull, wt, bcol, ocol, had, hadfull,
     local_sem, sz_send, sz_recv, sy_send, sy_recv, a_send, a_recv, b_send, b_recv,
@@ -78,16 +79,28 @@
     def greet(device):
         pl.semaphore_signal(barrier, inc=1, device_id=device, device_id_type=MESH)
 
+    ins = [
+        pltpu.make_async_copy(src, dst, local_sem.at[4 + n]) for n, (src, dst) in enumerate((
+            (embed_in, embed), (send_rows_in, sr_own), (w_in_in, w_in), (tile_rows_in, tile_rows),
+            (tile_cols_in, tile_cols), (src_local_in, src_local), (dst_owner_in, dst_owner),
+            (dst_local_in, dst_local), (b_in_in, b_in), (w_out_in, w_out),
+        ))
+    ]
+    ins[0].start()
+    ins[1].start()
     each(1, yc, lambda e: greet(at_a((j + e) % yc)))
     each(1, zc, lambda e: greet(at_b((k + e) % zc)))
     each(1, X, lambda e: greet(at_x((xf + e) % X)))
 
     fetch = pltpu.make_async_copy(weight_hbm.at[0], weight, local_sem.at[0])
+    for copy in ins[2:]:
+        copy.start()
     fetch.start()
+    ins[0].wait()
+    ins[1].wait()
     for r in range(RB):
         for h in range(2):
             cur0[h, r] = embed[h * half:(h + 1) * half, r * B:(r + 1) * B]
-    sr_own[...] = send_rows[...].reshape(1, parts)
 
     pl.semaphore_wait(barrier, yc - 1 + zc - 1 + X - 1)
 
@@ -178,7 +191,13 @@
             zs, ys = (z + Z - zigzag(zi, Z)) % Z, (y + Y - zigzag(yi, Y)) % Y
             for cs in range(C):
                 term(s * C + cs, jnp.concatenate([ra[ys * C + cs, zs], rb[zs * C + cs, ys]], axis=0))
-        total[parts + RB] = jnp.zeros(total.shape[1:], F32)
+        def corner(n, m):
+            pair(n * n + 2 * m, n, m)
+            pair(n * n + 2 * m + 1, m, n)
+        total[parts] = jnp.zeros(total.shape[1:], F32)
+        for r in range(RB):
+            block = jnp.concatenate([cur[0, r], cur[1, r]], axis=0)
+            own[r] = dot(block, weight[table_s[0, parts + r]], 1, 1)
         for n in range(Z):
             zs, ys = (z + Z - zigzag(n, Z)) % Z, (y + Y - zigzag(n, Y)) % Y
             if n > 0:
@@ -188,14 +207,17 @@
             elif C == 2:
                 end_a(y * C + 1 - c)
                 end_b(z * C + 1 - c)
-            each(0, n + 1, lambda m: pair(n * n + m, n, m))
-            if n > 0:
-                each(0, n, lambda m: pair(n * n + n + 1 + m, m, n))
-        for r in range(RB):
-            term(parts + r, jnp.concatenate([cur[0, r], cur[1, r]], axis=0))
+            def corners(m):
+                corner(n, 2 * m)
+                corner(n, 2 * m + 1)
+            each(0, n // 2, corners)
+            if n % 2 == 1:
+                corner(n, n - 1)
+            pair(n * n + 2 * n, n, n)
         for r in range(RB):
             first = jnp.concatenate([cur0[0, r], cur0[1, r]], axis=0).astype(F32)
-            new = ((1.0 - TELEPORT) * total[parts + r] + TELEPORT * first).astype(BF16)
+            summed = total[table_s[1, parts + r]] + own[r]
+            new = ((1.0 - TELEPORT) * summed + TELEPORT * first).astype(BF16)
             nxt[0, r] = new[:half]
             nxt[1, r] = new[half:]
 
@@ -209,10 +231,32 @@
     each(1, Y, rows_y)
     srz[z] = sr_own[...]
     sry[y] = sr_own[...]
+    ins[2].wait()
     each(1, X, lambda d: push(
         w_in, wfull.at[xf], wx_send.at[d], wx_recv.at[xf], at_x((xf + d) % X)).start())
     wfull[xf] = w_in[...]
 
+    def rows_z_end(d):
+        s = (z + d) % Z
+        push(sr_own, srz.at[s], rz_send.at[d], rz_recv.at[s], at_z(s)).wait_recv()
+    def rows_y_end(d):
+        s = (y + d) % Y
+        push(sr_own, sry.at[s], ry_send.at[d], ry_recv.at[s], at_y(s)).wait_recv()
+    each(1, Z, rows_z_end)
+    each(1, Y, rows_y_end)
+    rows_copies = [
+        pltpu.make_async_copy(srz, srz_s, local_sem.at[2]),
+        pltpu.make_async_copy(sry, sry_s, local_sem.at[3]),
+    ]
+    for copy in rows_copies:
+        copy.start()
+    for copy in rows_copies:
+        copy.wait()
+    shared(0, gz0, gy0)
+    deal(0, gz0, gy0, sa0, sb0, ra0, rb0)
+
+    for copy in ins[3:]:
+        copy.wait()
     slots = cols.shape[1]
     cols[...] = jnp.full(cols.shape, -1, I32)
     tiles = tile_cols.shape[1]
@@ -224,7 +268,7 @@
         return jnp.where(far == 0, 0, jnp.where(far <= n // 2, 2 * far - 1, 2 * (n - far)))
     zi = ring_place((z + Z - peer // yc) % Z, Z)
     yi = ring_place((y + Y - peer % yc // C) % Y, Y)
-    peer_slot = jnp.where(zi >= yi, zi * zi + yi, yi * yi + yi + 1 + zi) * C + peer % C
+    peer_slot = (jnp.maximum(zi, yi) * jnp.maximum(zi, yi) + 2 * jnp.minimum(zi, yi) + jnp.where(yi > zi, 1, 0)) * C + peer % C
     slot_of = jnp.where(col < 0, -1, jnp.where(col < RB, parts + col, peer_slot))
     hit = (iota((slots, slots), 0) == slot_of).astype(F32).astype(BF16)
     kind = iota((8, slots), 0)
@@ -238,7 +282,7 @@
     )
     last = jnp.max(before, axis=0, keepdims=True)
     table[0:1, :] = jnp.clip(found[0:1, :].astype(I32), 0, tiles - 1)
-    table[1:2, :] = jnp.clip(jnp.where(last < 0.0, float(parts + RB), last).astype(I32), 0, parts + RB)
+    table[1:2, :] = jnp.clip(jnp.where(last < 0.0, float(parts), last).astype(I32), 0, parts)
     to_smem = pltpu.make_async_copy(table, table_s, local_sem.at[1])
     to_smem.start()
 
@@ -264,37 +308,6 @@
         pick_slot[side] = (iota(pick_slot.shape[1:], 0) == spot_side).astype(F32).astype(BF16)
     pick_src[...] = (iota(pick_src.shape, 0) == src_local[...]).astype(F32).astype(BF16)
 
-    def rows_z_end(d):
-        s = (z + d) % Z
-        push(sr_own, srz.at[s], rz_send.at[d], rz_recv.at[s], at_z(s)).wait_recv()
-    def rows_y_end(d):
-        s = (y + d) % Y
-        push(sr_own, sry.at[s], ry_send.at[d], ry_recv.at[s], at_y(s)).wait_recv()
-    each(1, Z, rows_z_end)
-    each(1, Y, rows_y_end)
-    rows_copies = [
-        pltpu.make_async_copy(srz, srz_s, local_sem.at[2]),
-        pltpu.make_async_copy(sry, sry_s, local_sem.at[3]),
-    ]
-    for copy in rows_copies:
-        copy.start()
-    for copy in rows_copies:
-        copy.wait()
-    shared(0, gz0, gy0)
-    deal(0, gz0, gy0, sa0, sb0, ra0, rb0)
-
-    def ask_z_end(d):
-        s = (z + d) % Z
-        push(req.at[s], reqz.at[s], qz_send.at[d], qz_recv.at[s], at_z(s)).wait_recv()
-    each(1, Z, ask_z_end)
-    for jd in range(yc):
-        reqm[jd] = jnp.concatenate([reqz[s, jd:jd + 1, :] for s in range(Z)], axis=0)
-    def ask_y(e):
-        jd = (j + e) % yc
-        push(reqm.at[jd], reqy.at[j], qy_send.at[e], qy_recv.at[j], at_a(jd)).start()
-    each(1, yc, ask_y)
-    reqy[j] = reqm[j]
-
     def w_end(d):
         s = (xf + d) % X
         push(w_in, wfull.at[s], wx_send.at[d], wx_recv.at[s], at_x(s)).wait_recv()
@@ -313,6 +326,19 @@
     combine(0, cur0, sa0, sb0, ra0, rb0, cur1)
 
     share(1, cur1, gz1, gy1)
+
+    def ask_z_end(d):
+        s = (z + d) % Z
+        push(req.at[s], reqz.at[s], qz_send.at[d], qz_recv.at[s], at_z(s)).wait_recv()
+    each(1, Z, ask_z_end)
+    for jd in range(yc):
+        reqm[jd] = jnp.concatenate([reqz[s, jd:jd + 1, :] for s in range(Z)], axis=0)
+    def ask_y(e):
+        jd = (j + e) % yc
+        push(reqm.at[jd], reqy.at[j], qy_send.at[e], qy_recv.at[j], at_a(jd)).start()
+    each(1, yc, ask_y)
+    reqy[j] = reqm[j]
+
     shared(1, gz1, gy1)
     deal(1, gz1, gy1, sa1, sb1, ra1, rb1)
 
@@ -429,16 +455,21 @@
     cur = [V((2, RB, half, B), BF16)] * 3
     near = [V((n, RB, half, B), BF16) for n in (Z, Y, Z, Y)]
     deal = [V((n, m, half, B), BF16) for n, m in ((yc, Z), (zc, Y))]
-    scratch = cur + near + deal * 4 + [
-        V((tiles, B, B), BF16), V((parts + RB + 1, channels, B), F32),
+    staged = [
+        V((channels, nodes), BF16), V((1, tiles), I32), V((1, tiles), I32), V((1, parts), I32),
+        V((1, queries), I32), V((1, queries), I32), V((1, queries), I32),
+        V((channels, hidden), BF16), V((1, hidden), F32), V((1, hidden), F32),
+    ]
+    scratch = staged + cur + near + deal * 4 + [
+        V((tiles, B, B), BF16), V((parts + 1, channels, B), F32), V((RB, channels, B), F32),
         V((16, slots), I32), V((8, slots), I32), S((8, slots), I32),
-        V((1, parts), I32), V((Z, 1, parts), I32), V((Y, 1, parts), I32), S((Z, 1, parts), I32), S((Y, 1, parts), I32),
+        V((Z, 1, parts), I32), V((Y, 1, parts), I32), S((Z, 1, parts), I32), S((Y, 1, parts), I32),
         V((Z, yc, 128), I32), V((Z, yc, 128), I32), V((yc, Z, 128), I32), V((yc, Z, 128), I32),
         V((2, parts * fold, nodes), BF16), V((nodes, queries), BF16), V((2, parts * fold, queries), BF16),
         V((yc, Z, fold, 2 * channels), BF16), V((yc, Z, fold, 2 * channels), BF16), V((Z, yc, fold, 2 * channels), BF16),
         V((X, channels, hidden), BF16), V((hidden, X * channels), BF16), V((hidden, 128), F32), V((hidden, 128), F32),
         V((channels, queries), BF16), V((X, channels, queries), BF16),
-        D((4,)), D((HOPS, 2, Z // 2, 2)), D((HOPS, 2, Z // 2, 2)), D((HOPS, 2, Y // 2, 2)), D((HOPS, 2, Y // 2, 2)),
+        D((14,)), D((HOPS, 2, Z // 2, 2)), D((HOPS, 2, Z // 2, 2)), D((HOPS, 2, Y // 2, 2)), D((HOPS, 2, Y // 2, 2)),
         D((HOPS, yc)), D((HOPS, yc)), D((HOPS, zc)), D((HOPS, zc)),
         D((Z,)), D((Z,)), D((yc,)), D((yc,)), D((yc,)), D((yc,)), D((Z,)), D((Z,)),
         D((Z,)), D((Z,)), D((Y,)), D((Y,)), D((X,)), D((X,)), D((X,)), D((X,)),
@@ -450,7 +481,7 @@
             jax.ShapeDtypeStruct((channels, nodes), BF16),
             jax.ShapeDtypeStruct((1, queries), F32),
         ),
-        in_specs=[vmem, pl.BlockSpec(memory_space=pl.ANY)] + [vmem] * 9,
+        in_specs=[pl.BlockSpec(memory_space=pl.ANY)] * 11,
         out_specs=(vmem, vmem),
         scratch_shapes=scratch,
         compiler_params=pltpu.CompilerParams(

time: 134 us -> 126 us (0.940)
  Pallas kernels: 130 us -> 121 us
    pallas_call x1, Pallas kernels: 130 us -> 121 us  [shards(): pl.pallas_call(kernel, out_shape=(jax.ShapeDtypeStruct((channels, nodes),...]
where the time goes in v3:
time: 126 us; the launch traced here: 125 us
  Pallas kernels  121 us (96%)
  local copies, waits for them, and re-layouts  2.83 us (2%)
    pallas_call x1, Pallas kernels, shards(): pl.pallas_call(kernel, out_shape=(jax.ShapeDtypeStruct((channels, nodes),...  121 us
    unnamed x2, local copies, waits for them, and re-layouts  2.83 us

profile of v3, /device:TPU:1, one launch (start us, length us, event | category | flops | bytes accessed | tf_op | source)
XLA Modules:
  0.0 124.6 jit_solution(7059149897844569980)
XLA Ops:
  0.6 121.1 %shard_map.122 = (bf16[64,1024]{1,0:T(8,128)(2,1)}, f32[1,512]{1,0:T(1,128)}) custom-call(bf16[64,1024]{1,0:T(8,128)(2,1)} %embed_in.1, bf16[1,135,128,128]{3,2,1,0:T(8,128)(2,1)} %weight_hbm.1, s32[1,135]{1,0:T(1,128)} %tile_rows_in.1, s32[1,135]{1,0:T(1,128)} %tile_cols_in.1, s32[1,128]{1,0:T(1,128)} %send_rows_in.1, s32[1,512]{1,0:T(1,128)} %bitcast.8, ...), custom_call_target="tpu_custom_call" | custom-call | tf_op jit(solution)/shard_map/pallas_call | solution.py:478
  121.8 1.6 %copy.15 = bf16[64,1024]{1,0:T(8,128)(2,1)} copy(bf16[64,1024]{1,0:T(8,128)(2,1)} %get-tuple-element.8) | data formatting | bytes 262144
  123.3 1.3 %copy.16 = f32[512]{0:T(512)} copy(f32[512]{0:T(512)} %bitcast.11) | data formatting | bytes 4096

commit v4 on v3

--- a/solution.py
+++ b/solution.py
@@ -27,7 +27,7 @@
     embed_in, weight_hbm, tile_rows_in, tile_cols_in, send_rows_in, src_local_in, dst_owner_in, dst_local_in,
     w_in_in, b_in_in, w_out_in, out, scores,
     embed, tile_rows, tile_cols, sr_own, src_local, dst_owner, dst_local, w_in, b_in, w_out,
-    cur0, cur1, cur2, gz0, gy0, gz1, gy1, sa0, sb0, sa1, sb1, ra0, rb0, ra1, rb1,
+    cur0, cur1, cur2, gz0, gy0, gz1, gy1, fz0, fy0, fz1, fy1, sa0, sb0, sa1, sb1, ra0, rb0, ra1, rb1,
     weight, total, own, cols, table, table_s, srz, sry, srz_s, sry_s,
     req, reqz, reqm, reqy, pick, pick_src, pick_slot, reply, mid, got,
     wfull, wt, bcol, ocol, had, hadfull,
@@ -104,68 +104,59 @@
 
     pl.semaphore_wait(barrier, yc - 1 + zc - 1 + X - 1)
 
-    def ring_copies(hop, gz, gy, step, piece, way):
-        rows = pl.ds(piece * (RB // 2), RB // 2)
-        sz, sy = (z - way * step) % Z, (y - way * step) % Y
+    steps = Z // 2
+    near = min(5, Z)
+    groups = [(0, near)] + ([(near, Z)] if near < Z else [])
+    early = [(d, way) for d in range(1, min(2, steps) + 1) for way in (1, -1)]
+    late = [(d, way) for d in range(3, steps + 1) for way in (1, -1)]
+
+    def ring_slot(distance, way):
+        return 0 if distance == 0 else 2 * distance - 1 if way == 1 or distance == steps else 2 * distance
+
+    def at_place(near_ref, far_ref, n, rows):
+        return near_ref.at[n, rows] if n < near else far_ref.at[n - near, rows]
+
+    def ring_copies(hop, gz, gy, fz, fy, d, way):
         side = 0 if way == 1 else 1
+        rows = pl.ds(side * (RB // 2), RB // 2) if d == steps else pl.ds(0, RB)
+        start = 0 if d <= 2 else 2
+        here, there = ring_slot(start, way), ring_slot(d, way)
+        move = way * (d - start)
         return (
-            push(gz.at[sz, rows], gz.at[sz, rows], sz_send.at[hop, side, step, piece],
-                 sz_recv.at[hop, side, step, piece], at_z((z + way) % Z)),
-            push(gy.at[sy, rows], gy.at[sy, rows], sy_send.at[hop, side, step, piece],
-                 sy_recv.at[hop, side, step, piece], at_y((y + way) % Y)),
+            push(at_place(gz, fz, here, rows), at_place(gz, fz, there, rows), sz_send.at[hop, side, d - 1],
+                 sz_recv.at[hop, side, d - 1], at_z((z + Z + move) % Z)),
+            push(at_place(gy, fy, here, rows), at_place(gy, fy, there, rows), sy_send.at[hop, side, d - 1],
+                 sy_recv.at[hop, side, d - 1], at_y((y + Y + move) % Y)),
         )
 
-    ring = [
-        (step, piece, way)
-        for step in range(Z // 2) for piece in range(2) for way in (1, -1)
-        if step < Z // 2 - 1 or piece == (0 if way == 1 else 1)
-    ]
-
-    def arrived(hop, gz, gy, step, piece, way):
-        rows = pl.ds(piece * (RB // 2), RB // 2)
-        sz, sy = (z - way * (step + 1)) % Z, (y - way * (step + 1)) % Y
-        side = 0 if way == 1 else 1
-        push(gz.at[sz, rows], gz.at[sz, rows], sz_send.at[hop, side, step, piece],
-             sz_recv.at[hop, side, step, piece], at_z((z + way) % Z)).wait_recv()
-        push(gy.at[sy, rows], gy.at[sy, rows], sy_send.at[hop, side, step, piece],
-             sy_recv.at[hop, side, step, piece], at_y((y + way) % Y)).wait_recv()
-
-    def share(hop, cur, gz, gy):
-        gz[z] = cur[0]
-        gy[y] = cur[1]
-        for step, piece, way in ring:
-            if step == 0:
-                for copy in ring_copies(hop, gz, gy, step, piece, way):
-                    copy.start()
-
-    def shared(hop, gz, gy):
-        passed = set()
-        for step, piece, way in ring:
-            if step > 0:
-                arrived(hop, gz, gy, step - 1, piece, way)
-                passed.add((step - 1, piece, way))
-                for copy in ring_copies(hop, gz, gy, step, piece, way):
-                    copy.start()
-        for one in ring:
-            if one not in passed:
-                arrived(hop, gz, gy, *one)
-
-    def deal(hop, gz, gy, sa, sb, ra, rb):
+    def ring_go(bufs, moves):
+        for one in moves:
+            for copy in ring_copies(*bufs, *one):
+                copy.start()
+
+    def ring_end(bufs, moves):
+        for one in moves:
+            for copy in ring_copies(*bufs, *one):
+                copy.wait_recv()
+
+    def deal(hop, group, z_from, y_from, sa, sb, ra, rb):
+        lo, hi = groups[group]
         def fill_a(jd, dst):
-            for s in range(Z):
-                dst[jd, s] = gz[s, srz_s[s, 0, z * yc + jd]]
+            for n in range(lo, hi):
+                s = (z + Z - zigzag(n, Z)) % Z
+                dst[jd, n] = z_from[n - lo, srz_s[s, 0, z * yc + jd]]
         def fill_b(kd, dst):
-            for s in range(Y):
-                dst[kd, s] = gy[s, sry_s[s, 0, ((kd // C) * Y + y) * C + kd % C]]
+            for n in range(lo, hi):
+                s = (y + Y - zigzag(n, Y)) % Y
+                dst[kd, n] = y_from[n - lo, sry_s[s, 0, ((kd // C) * Y + y) * C + kd % C]]
         def go_a(jd):
             fill_a(jd, sa)
-            push(sa.at[jd], ra.at[j], a_send.at[hop, jd], a_recv.at[hop, j], at_a(jd)).start()
+            copy_a(hop, group, sa, ra, jd, j).start()
         def go_b(kd):
             fill_b(kd, sb)
-            push(sb.at[kd], rb.at[k], b_send.at[hop, kd], b_recv.at[hop, k], at_b(kd)).start()
-        fill_a(j, ra)
-        fill_b(k, rb)
+            copy_b(hop, group, sb, rb, kd, k).start()
         def ring_step(i):
+            i = Y - 1 - i
             if C == 2:
                 @pl.when(i == 0)
                 def _():
@@ -178,19 +169,49 @@
                     go_a(yd * C + cd)
                     go_b(zd * C + cd)
         each(0, Y, ring_step)
+        fill_a(j, ra)
+        fill_b(k, rb)
+
+    def copy_a(hop, group, sa, ra, there, here):
+        lo, hi = groups[group]
+        span = pl.ds(lo, hi - lo)
+        return push(sa.at[there, span], ra.at[here, span], a_send.at[hop, group, there],
+                    a_recv.at[hop, group, here], at_a(there))
+
+    def copy_b(hop, group, sb, rb, there, here):
+        lo, hi = groups[group]
+        span = pl.ds(lo, hi - lo)
+        return push(sb.at[there, span], rb.at[here, span], b_send.at[hop, group, there],
+                    b_recv.at[hop, group, here], at_b(there))
+
+    def begin(hop, cur, gz, gy, fz, fy):
+        gz[0] = cur[0]
+        gy[0] = cur[1]
+        ring_go((hop, gz, gy, fz, fy), early)
+
+    def exchange(hop, gz, gy, fz, fy, sa, sb, ra, rb, before_deal):
+        bufs = (hop, gz, gy, fz, fy)
+        ring_end(bufs, early)
+        ring_go(bufs, late)
+        before_deal()
+        deal(hop, 0, gz, gy, sa, sb, ra, rb)
+        if late:
+            ring_end(bufs, late)
+            deal(hop, 1, fz, fy, sa, sb, ra, rb)
 
     def combine(hop, cur, sa, sb, ra, rb, nxt):
-        def end_a(s):
-            push(sa.at[s], ra.at[s], a_send.at[hop, s], a_recv.at[hop, s], at_a(s)).wait_recv()
-        def end_b(s):
-            push(sb.at[s], rb.at[s], b_send.at[hop, s], b_recv.at[hop, s], at_b(s)).wait_recv()
+        def end(group, n):
+            zs, ys = (z + Z - zigzag(n, Z)) % Z, (y + Y - zigzag(n, Y)) % Y
+            for cs in range(C) if n > 0 else ([1 - c] if C == 2 else []):
+                copy_a(hop, group, sa, ra, ys * C + cs, ys * C + cs).wait_recv()
+                copy_b(hop, group, sb, rb, zs * C + cs, zs * C + cs).wait_recv()
         def term(s, block):
             product = dot(block, weight[table_s[0, s]], 1, 1)
             total[s] = product + total[table_s[1, s]]
         def pair(s, zi, yi):
             zs, ys = (z + Z - zigzag(zi, Z)) % Z, (y + Y - zigzag(yi, Y)) % Y
             for cs in range(C):
-                term(s * C + cs, jnp.concatenate([ra[ys * C + cs, zs], rb[zs * C + cs, ys]], axis=0))
+                term(s * C + cs, jnp.concatenate([ra[ys * C + cs, zi], rb[zs * C + cs, yi]], axis=0))
         def corner(n, m):
             pair(n * n + 2 * m, n, m)
             pair(n * n + 2 * m + 1, m, n)
@@ -198,15 +219,13 @@
         for r in range(RB):
             block = jnp.concatenate([cur[0, r], cur[1, r]], axis=0)
             own[r] = dot(block, weight[table_s[0, parts + r]], 1, 1)
+        ended = set()
         for n in range(Z):
-            zs, ys = (z + Z - zigzag(n, Z)) % Z, (y + Y - zigzag(n, Y)) % Y
-            if n > 0:
-                for cs in range(C):
-                    end_a(ys * C + cs)
-                    end_b(zs * C + cs)
-            elif C == 2:
-                end_a(y * C + 1 - c)
-                end_b(z * C + 1 - c)
+            for group in range(1 if n < near else 2):
+                for m in range(n + 1):
+                    if (group, m) not in ended:
+                        end(group, m)
+                        ended.add((group, m))
             def corners(m):
                 corner(n, 2 * m)
                 corner(n, 2 * m + 1)
@@ -221,7 +240,6 @@
             nxt[0, r] = new[:half]
             nxt[1, r] = new[half:]
 
-    share(0, cur0, gz0, gy0)
 
     def rows_z(d):
         push(sr_own, srz.at[z], rz_send.at[d], rz_recv.at[z], at_z((z + d) % Z)).start()
@@ -231,29 +249,30 @@
     each(1, Y, rows_y)
     srz[z] = sr_own[...]
     sry[y] = sr_own[...]
+    begin(0, cur0, gz0, gy0, fz0, fy0)
     ins[2].wait()
     each(1, X, lambda d: push(
         w_in, wfull.at[xf], wx_send.at[d], wx_recv.at[xf], at_x((xf + d) % X)).start())
     wfull[xf] = w_in[...]
 
-    def rows_z_end(d):
-        s = (z + d) % Z
-        push(sr_own, srz.at[s], rz_send.at[d], rz_recv.at[s], at_z(s)).wait_recv()
-    def rows_y_end(d):
-        s = (y + d) % Y
-        push(sr_own, sry.at[s], ry_send.at[d], ry_recv.at[s], at_y(s)).wait_recv()
-    each(1, Z, rows_z_end)
-    each(1, Y, rows_y_end)
-    rows_copies = [
-        pltpu.make_async_copy(srz, srz_s, local_sem.at[2]),
-        pltpu.make_async_copy(sry, sry_s, local_sem.at[3]),
-    ]
-    for copy in rows_copies:
-        copy.start()
-    for copy in rows_copies:
-        copy.wait()
-    shared(0, gz0, gy0)
-    deal(0, gz0, gy0, sa0, sb0, ra0, rb0)
+    def rows_ready():
+        def rows_z_end(d):
+            s = (z + d) % Z
+            push(sr_own, srz.at[s], rz_send.at[d], rz_recv.at[s], at_z(s)).wait_recv()
+        def rows_y_end(d):
+            s = (y + d) % Y
+            push(sr_own, sry.at[s], ry_send.at[d], ry_recv.at[s], at_y(s)).wait_recv()
+        each(1, Z, rows_z_end)
+        each(1, Y, rows_y_end)
+        rows_copies = [
+            pltpu.make_async_copy(srz, srz_s, local_sem.at[2]),
+            pltpu.make_async_copy(sry, sry_s, local_sem.at[3]),
+        ]
+        for copy in rows_copies:
+            copy.start()
+        for copy in rows_copies:
+            copy.wait()
+    exchange(0, gz0, gy0, fz0, fy0, sa0, sb0, ra0, rb0, rows_ready)
 
     for copy in ins[3:]:
         copy.wait()
@@ -325,7 +344,7 @@
     fetch.wait()
     combine(0, cur0, sa0, sb0, ra0, rb0, cur1)
 
-    share(1, cur1, gz1, gy1)
+    begin(1, cur1, gz1, gy1, fz1, fy1)
 
     def ask_z_end(d):
         s = (z + d) % Z
@@ -339,8 +358,7 @@
     each(1, yc, ask_y)
     reqy[j] = reqm[j]
 
-    shared(1, gz1, gy1)
-    deal(1, gz1, gy1, sa1, sb1, ra1, rb1)
+    exchange(1, gz1, gy1, fz1, fy1, sa1, sb1, ra1, rb1, lambda: None)
 
     def ask_y_end(e):
         s = (j + e) % yc
@@ -408,18 +426,18 @@
         score = score + jnp.sum(active.reshape(16, 8, queries), axis=0)
     scores[...] = jnp.sum(score, axis=0, keepdims=True)
 
-    for hop, gz, gy, sa, sb, ra, rb in (
-        (0, gz0, gy0, sa0, sb0, ra0, rb0), (1, gz1, gy1, sa1, sb1, ra1, rb1)
+    for hop, gz, gy, fz, fy, sa, sb, ra, rb in (
+        (0, gz0, gy0, fz0, fy0, sa0, sb0, ra0, rb0), (1, gz1, gy1, fz1, fy1, sa1, sb1, ra1, rb1)
     ):
-        for one in ring:
-            for copy in ring_copies(hop, gz, gy, *one):
+        for one in early + late:
+            for copy in ring_copies(hop, gz, gy, fz, fy, *one):
                 copy.wait_send()
         def left_a(e):
-            jd = (j + e) % yc
-            push(sa.at[jd], ra.at[j], a_send.at[hop, jd], a_recv.at[hop, j], at_a(jd)).wait_send()
+            for group in range(len(groups)):
+                copy_a(hop, group, sa, ra, (j + e) % yc, j).wait_send()
         def left_b(e):
-            kd = (k + e) % zc
-            push(sb.at[kd], rb.at[k], b_send.at[hop, kd], b_recv.at[hop, k], at_b(kd)).wait_send()
+            for group in range(len(groups)):
+                copy_b(hop, group, sb, rb, (k + e) % zc, k).wait_send()
         each(1, yc, left_a)
         each(1, zc, left_b)
     def left_z(d):
@@ -453,7 +471,8 @@
     slots, fold = 256, CAP // 2
     V, S, D = pltpu.VMEM, pltpu.SMEM, pltpu.SemaphoreType.DMA
     cur = [V((2, RB, half, B), BF16)] * 3
-    near = [V((n, RB, half, B), BF16) for n in (Z, Y, Z, Y)]
+    near = [V((min(5, n), RB, half, B), BF16) for n in (Z, Y, Z, Y)]
+    near += [V((max(1, n - 5), RB, half, B), BF16) for n in (Z, Y, Z, Y)]
     deal = [V((n, m, half, B), BF16) for n, m in ((yc, Z), (zc, Y))]
     staged = [
         V((channels, nodes), BF16), V((1, tiles), I32), V((1, tiles), I32), V((1, parts), I32),
@@ -469,8 +488,8 @@
         V((yc, Z, fold, 2 * channels), BF16), V((yc, Z, fold, 2 * channels), BF16), V((Z, yc, fold, 2 * channels), BF16),
         V((X, channels, hidden), BF16), V((hidden, X * channels), BF16), V((hidden, 128), F32), V((hidden, 128), F32),
         V((channels, queries), BF16), V((X, channels, queries), BF16),
-        D((14,)), D((HOPS, 2, Z // 2, 2)), D((HOPS, 2, Z // 2, 2)), D((HOPS, 2, Y // 2, 2)), D((HOPS, 2, Y // 2, 2)),
-        D((HOPS, yc)), D((HOPS, yc)), D((HOPS, zc)), D((HOPS, zc)),
+        D((14,)), D((HOPS, 2, Z // 2)), D((HOPS, 2, Z // 2)), D((HOPS, 2, Y // 2)), D((HOPS, 2, Y // 2)),
+        D((HOPS, 2, yc)), D((HOPS, 2, yc)), D((HOPS, 2, zc)), D((HOPS, 2, zc)),
         D((Z,)), D((Z,)), D((yc,)), D((yc,)), D((yc,)), D((yc,)), D((Z,)), D((Z,)),
         D((Z,)), D((Z,)), D((Y,)), D((Y,)), D((X,)), D((X,)), D((X,)), D((X,)),
     ]

time: 126 us -> 119 us (0.944)
  Pallas kernels: 121 us -> 115 us
    pallas_call x1, Pallas kernels: 121 us -> 115 us  [shards(): pl.pallas_call(kernel, out_shape=(jax.ShapeDtypeStruct((channels, nodes),...]
where the time goes in v4:
time: 119 us
  Pallas kernels  115 us (97%)
  local copies, waits for them, and re-layouts  2.83 us (2%)
    pallas_call x1, Pallas kernels, shards(): pl.pallas_call(kernel, out_shape=(jax.ShapeDtypeStruct((channels, nodes),...  115 us
    unnamed x2, local copies, waits for them, and re-layouts  2.83 us

profile of v4, /device:TPU:1, one launch (start us, length us, event | category | flops | bytes accessed | tf_op | source)
XLA Modules:
  0.0 118.5 jit_solution(17807429502622078935)
XLA Ops:
  0.6 115.1 %shard_map.122 = (bf16[64,1024]{1,0:T(8,128)(2,1)}, f32[1,512]{1,0:T(1,128)}) custom-call(bf16[64,1024]{1,0:T(8,128)(2,1)} %embed_in.1, bf16[1,135,128,128]{3,2,1,0:T(8,128)(2,1)} %weight_hbm.1, s32[1,135]{1,0:T(1,128)} %tile_rows_in.1, s32[1,135]{1,0:T(1,128)} %tile_cols_in.1, s32[1,128]{1,0:T(1,128)} %send_rows_in.1, s32[1,512]{1,0:T(1,128)} %bitcast.8, ...), custom_call_target="tpu_custom_call" | custom-call | tf_op jit(solution)/shard_map/pallas_call | solution.py:497
  115.7 1.6 %copy.15 = bf16[64,1024]{1,0:T(8,128)(2,1)} copy(bf16[64,1024]{1,0:T(8,128)(2,1)} %get-tuple-element.8) | data formatting | bytes 262144
  117.3 1.3 %copy.16 = f32[512]{0:T(512)} copy(f32[512]{0:T(512)} %bitcast.11) | data formatting | bytes 4096

commit v5 on v4

--- a/solution.py
+++ b/solution.py
@@ -29,10 +29,11 @@
     embed, tile_rows, tile_cols, sr_own, src_local, dst_owner, dst_local, w_in, b_in, w_out,
     cur0, cur1, cur2, gz0, gy0, gz1, gy1, fz0, fy0, fz1, fy1, sa0, sb0, sa1, sb1, ra0, rb0, ra1, rb1,
     weight, total, own, cols, table, table_s, srz, sry, srz_s, sry_s,
-    req, reqz, reqm, reqy, pick, pick_src, pick_slot, reply, mid, got,
+    req, reqz, reqm, reqy, pick, pick_src, pick_slot, reply, mid, got, reply2, mid2, got2,
     wfull, wt, bcol, ocol, had, hadfull,
     local_sem, sz_send, sz_recv, sy_send, sy_recv, a_send, a_recv, b_send, b_recv,
     qz_send, qz_recv, qy_send, qy_recv, pa_send, pa_recv, pb_send, pb_recv,
+    pc_send, pc_recv, pd_send, pd_recv,
     rz_send, rz_recv, ry_send, ry_recv, wx_send, wx_recv, hx_send, hx_recv,
 ):
     parts = Z * Y * C
@@ -321,7 +322,13 @@
     each(1, Z, ask_z)
     reqz[z] = req[z]
     fold = CAP // 2
-    spot = owner * fold + rank % fold
+    duo = fold // 2
+    owner_z, owner_y, owner_c = owner // yc, owner % yc // C, owner % C
+    turn = rank % fold
+    spot = jnp.where(
+        turn < duo, owner * duo + turn,
+        parts * duo + (owner_y * zc + owner_z * C + owner_c) * duo + turn - duo,
+    )
     for side in range(2):
         spot_side = jnp.where(rank // fold == side, spot, -1)
         pick_slot[side] = (iota(pick_slot.shape[1:], 0) == spot_side).astype(F32).astype(BF16)
@@ -365,12 +372,16 @@
         push(reqm.at[s], reqy.at[s], qy_send.at[e], qy_recv.at[s], at_a(s)).wait_recv()
     each(1, yc, ask_y_end)
     asked = reqy[...].reshape(parts, 128).astype(F32)
-    spread = (iota((parts * fold, parts), 0) // fold == iota((parts * fold, parts), 1)).astype(F32)
+    row = iota((parts * fold, 1), 0)
+    row2 = row - parts * duo
+    asker = jnp.where(row2 < 0, row // duo, ((row2 // duo % Y) * C + row2 // (duo * Y) % C) * Z + row2 // (duo * Y * C))
+    lane = row % duo + jnp.where(row2 < 0, 0, duo)
+    spread = (asker == iota((parts * fold, parts), 1)).astype(F32)
     wide = lax.dot_general(
         spread, asked, (((1,), (0,)), ((), ())), precision=lax.Precision.HIGHEST, preferred_element_type=F32
     )
     for side in range(2):
-        mine = iota(wide.shape, 1) == iota(wide.shape, 0) % fold + side * fold
+        mine = iota(wide.shape, 1) == lane + side * fold
         node = jnp.sum(jnp.where(mine, wide, 0.0), axis=1, keepdims=True).astype(I32)
         pick[side] = (iota((parts * fold, nodes), 1) == node).astype(F32).astype(BF16)
 
@@ -381,12 +392,18 @@
 
     final = out[...]
     rows = jnp.concatenate([dot(pick[side], final, 1, 1) for side in range(2)], axis=1)
-    reply[...] = rows.reshape(yc, Z, fold, 2 * channels).astype(BF16)
+    reply[...] = rows[:parts * duo].reshape(yc, Z, duo, 2 * channels).astype(BF16)
+    reply2[...] = rows[parts * duo:].reshape(zc, Y, duo, 2 * channels).astype(BF16)
     def reply_a(i):
         jd = (j + i) % yc
         push(reply.at[jd], mid.at[j], pa_send.at[i], pa_recv.at[j], at_a(jd)).start()
     each(1, yc, reply_a)
+    def reply_b(i):
+        kd = (k + i) % zc
+        push(reply2.at[kd], mid2.at[k], pc_send.at[i], pc_recv.at[k], at_b(kd)).start()
+    each(1, zc, reply_b)
     mid[j] = reply[j]
+    mid2[k] = reply2[k]
     source = dot(final, pick_src[...], 1, 0)
     def reply_a_end(e):
         s = (j + e) % yc
@@ -396,12 +413,27 @@
         zd = (z + d) % Z
         push(mid.at[:, zd], got.at[z], pb_send.at[d], pb_recv.at[z], at_z(zd)).start()
     each(1, Z, reply_z)
+    def reply_b_end(e):
+        s = (k + e) % zc
+        push(reply2.at[s], mid2.at[s], pc_send.at[e], pc_recv.at[s], at_b(s)).wait_recv()
+    each(1, zc, reply_b_end)
+    def reply_y(d):
+        yd = (y + d) % Y
+        push(mid2.at[:, yd], got2.at[y], pd_send.at[d], pd_recv.at[y], at_y(yd)).start()
+    each(1, Y, reply_y)
     got[z] = mid[:, z]
+    got2[y] = mid2[:, y]
     def reply_z_end(d):
         s = (z + d) % Z
         push(mid.at[:, s], got.at[s], pb_send.at[d], pb_recv.at[s], at_z(s)).wait_recv()
     each(1, Z, reply_z_end)
-    replies = got[...].reshape(parts * fold, 2 * channels)
+    def reply_y_end(d):
+        s = (y + d) % Y
+        push(mid2.at[:, s], got2.at[s], pd_send.at[d], pd_recv.at[s], at_y(s)).wait_recv()
+    each(1, Y, reply_y_end)
+    replies = jnp.concatenate(
+        [half_got[...].reshape(parts * duo, 2 * channels) for half_got in (got, got2)], axis=0
+    )
     target = dot(replies, pick_slot[0], 0, 0)[:channels] + dot(replies, pick_slot[1], 0, 0)[channels:]
     had[...] = (source * target).astype(BF16)
     def had_x(d):
@@ -453,11 +485,20 @@
         push(reqm.at[jd], reqy.at[j], qy_send.at[e], qy_recv.at[j], at_a(jd)).wait_send()
         push(reply.at[jd], mid.at[j], pa_send.at[e], pa_recv.at[j], at_a(jd)).wait_send()
     each(1, yc, left_y)
+    each(1, zc, lambda i: push(
+        reply2.at[(k + i) % zc], mid2.at[k], pc_send.at[i], pc_recv.at[k], at_b((k + i) % zc)).wait_send())
+    each(1, Y, lambda d: push(
+        mid2.at[:, (y + d) % Y], got2.at[y], pd_send.at[d], pd_recv.at[y], at_y((y + d) % Y)).wait_send())
     def left_x(d):
         xd = (xf + d) % X
         push(w_in, wfull.at[xf], wx_send.at[d], wx_recv.at[xf], at_x(xd)).wait_send()
         push(had, hadfull.at[xf], hx_send.at[d], hx_recv.at[xf], at_x(xd)).wait_send()
     each(1, X, left_x)
+
+
+def finish(out_in, scores_in, out, scores):
+    out[...] = out_in[...]
+    scores[...] = scores_in[...]
 
 
 def shards(
@@ -468,7 +509,7 @@
     half = channels // 2
     queries, hidden = src_local.shape[0], w_in.shape[1]
     tiles = tile_rows.shape[1]
-    slots, fold = 256, CAP // 2
+    slots, fold, duo = 256, CAP // 2, CAP // 4
     V, S, D = pltpu.VMEM, pltpu.SMEM, pltpu.SemaphoreType.DMA
     cur = [V((2, RB, half, B), BF16)] * 3
     near = [V((min(5, n), RB, half, B), BF16) for n in (Z, Y, Z, Y)]
@@ -485,12 +526,14 @@
         V((Z, 1, parts), I32), V((Y, 1, parts), I32), S((Z, 1, parts), I32), S((Y, 1, parts), I32),
         V((Z, yc, 128), I32), V((Z, yc, 128), I32), V((yc, Z, 128), I32), V((yc, Z, 128), I32),
         V((2, parts * fold, nodes), BF16), V((nodes, queries), BF16), V((2, parts * fold, queries), BF16),
-        V((yc, Z, fold, 2 * channels), BF16), V((yc, Z, fold, 2 * channels), BF16), V((Z, yc, fold, 2 * channels), BF16),
+        V((yc, Z, duo, 2 * channels), BF16), V((yc, Z, duo, 2 * channels), BF16), V((Z, yc, duo, 2 * channels), BF16),
+        V((zc, Y, duo, 2 * channels), BF16), V((zc, Y, duo, 2 * channels), BF16), V((Y, zc, duo, 2 * channels), BF16),
         V((X, channels, hidden), BF16), V((hidden, X * channels), BF16), V((hidden, 128), F32), V((hidden, 128), F32),
         V((channels, queries), BF16), V((X, channels, queries), BF16),
         D((14,)), D((HOPS, 2, Z // 2)), D((HOPS, 2, Z // 2)), D((HOPS, 2, Y // 2)), D((HOPS, 2, Y // 2)),
         D((HOPS, 2, yc)), D((HOPS, 2, yc)), D((HOPS, 2, zc)), D((HOPS, 2, zc)),
         D((Z,)), D((Z,)), D((yc,)), D((yc,)), D((yc,)), D((yc,)), D((Z,)), D((Z,)),
+        D((zc,)), D((zc,)), D((Y,)), D((Y,)),
         D((Z,)), D((Z,)), D((Y,)), D((Y,)), D((X,)), D((X,)), D((X,)), D((X,)),
     ]
     vmem = pl.BlockSpec(memory_space=pltpu.VMEM)
@@ -511,6 +554,15 @@
         src_local.reshape(1, queries), dst_owner.reshape(1, queries), dst_local.reshape(1, queries),
         w_in, b_in.reshape(1, hidden), w_out.reshape(1, hidden),
     )
+    propagated, scores = pl.pallas_call(
+        finish,
+        out_shape=(
+            jax.ShapeDtypeStruct((channels, nodes), BF16),
+            jax.ShapeDtypeStruct((1, queries), F32),
+        ),
+        in_specs=[vmem] * 2,
+        out_specs=(vmem, vmem),
+    )(propagated, scores)
     return propagated, scores.reshape(queries)
 
 

time: 119 us -> 117 us (0.983)
  local copies, waits for them, and re-layouts: 2.83 us -> 0 us
    unnamed x2 -> x0, local copies, waits for them, and re-layouts: 2.83 us -> none
    pallas_call x0 -> x1, Pallas kernels: none -> 1.57 us  [shards(): pl.pallas_call(finish, out_shape=(jax.ShapeDtypeStruct((channels, nodes),...]
where the time goes in v5:
time: 117 us
  Pallas kernels  116 us (99%)
    pallas_call x1, Pallas kernels, shards(): pl.pallas_call(kernel, out_shape=(jax.ShapeDtypeStruct((channels, nodes),...  114 us

profile of v5, /device:TPU:1, one launch (start us, length us, event | category | flops | bytes accessed | tf_op | source)
XLA Modules:
  0.0 116.7 jit_solution(10756011375382525734)
XLA Ops:
  0.6 114.5 %shard_map.122 = (bf16[64,1024]{1,0:T(8,128)(2,1)}, f32[1,512]{1,0:T(1,128)}) custom-call(bf16[64,1024]{1,0:T(8,128)(2,1)} %embed_in.1, bf16[1,135,128,128]{3,2,1,0:T(8,128)(2,1)} %weight_hbm.1, s32[1,135]{1,0:T(1,128)} %tile_rows_in.1, s32[1,135]{1,0:T(1,128)} %tile_cols_in.1, s32[1,128]{1,0:T(1,128)} %send_rows_in.1, s32[1,512]{1,0:T(1,128)} %bitcast.8, ...), custom_call_target="tpu_custom_call" | custom-call | tf_op jit(solution)/shard_map/pallas_call | solution.py:540
  115.1 1.6 %shard_map.123 = (bf16[64,1024]{1,0:T(8,128)(2,1)}, f32[1,512]{1,0:T(1,128)}) custom-call(bf16[64,1024]{1,0:T(8,128)(2,1)} %get-tuple-element.6.out_in, f32[1,512]{1,0:T(1,128)} %get-tuple-element.7.scores_in), custom_call_target="tpu_custom_call" | custom-call | tf_op jit(solution)/shard_map/pallas_call | solution.py:557

commit v6 on v5

--- a/solution.py
+++ b/solution.py
@@ -199,6 +199,19 @@
         if late:
             ring_end(bufs, late)
             deal(hop, 1, fz, fy, sa, sb, ra, rb)
+
+    def drain(hop, gz, gy, fz, fy, sa, sb, ra, rb):
+        for one in early + late:
+            for copy in ring_copies(hop, gz, gy, fz, fy, *one):
+                copy.wait_send()
+        def left_a(e):
+            for group in range(len(groups)):
+                copy_a(hop, group, sa, ra, (j + e) % yc, j).wait_send()
+        def left_b(e):
+            for group in range(len(groups)):
+                copy_b(hop, group, sb, rb, (k + e) % zc, k).wait_send()
+        each(1, yc, left_a)
+        each(1, zc, left_b)
 
     def combine(hop, cur, sa, sb, ra, rb, nxt):
         def end(group, n):
@@ -367,6 +380,8 @@
 
     exchange(1, gz1, gy1, fz1, fy1, sa1, sb1, ra1, rb1, lambda: None)
 
+    drain(0, gz0, gy0, fz0, fy0, sa0, sb0, ra0, rb0)
+
     def ask_y_end(e):
         s = (j + e) % yc
         push(reqm.at[s], reqy.at[s], qy_send.at[e], qy_recv.at[s], at_a(s)).wait_recv()
@@ -405,6 +420,7 @@
     mid[j] = reply[j]
     mid2[k] = reply2[k]
     source = dot(final, pick_src[...], 1, 0)
+    drain(1, gz1, gy1, fz1, fy1, sa1, sb1, ra1, rb1)
     def reply_a_end(e):
         s = (j + e) % yc
         push(reply.at[s], mid.at[s], pa_send.at[e], pa_recv.at[s], at_a(s)).wait_recv()
@@ -458,20 +474,6 @@
         score = score + jnp.sum(active.reshape(16, 8, queries), axis=0)
     scores[...] = jnp.sum(score, axis=0, keepdims=True)
 
-    for hop, gz, gy, fz, fy, sa, sb, ra, rb in (
-        (0, gz0, gy0, fz0, fy0, sa0, sb0, ra0, rb0), (1, gz1, gy1, fz1, fy1, sa1, sb1, ra1, rb1)
-    ):
-        for one in early + late:
-            for copy in ring_copies(hop, gz, gy, fz, fy, *one):
-                copy.wait_send()
-        def left_a(e):
-            for group in range(len(groups)):
-                copy_a(hop, group, sa, ra, (j + e) % yc, j).wait_send()
-        def left_b(e):
-            for group in range(len(groups)):
-                copy_b(hop, group, sb, rb, (k + e) % zc, k).wait_send()
-        each(1, yc, left_a)
-        each(1, zc, left_b)
     def left_z(d):
         zd = (z + d) % Z
         push(sr_own, srz.at[z], rz_send.at[d], rz_recv.at[z], at_z(zd)).wait_send()

time: 117 us -> 116 us (level)
  no operation moved by 1% of the time
where the time goes in v6:
time: 116 us
  Pallas kernels  115 us (99%)
    pallas_call x1, Pallas kernels, shards(): pl.pallas_call(kernel, out_shape=(jax.ShapeDtypeStruct((channels, nodes),...  113 us

profile of v6, /device:TPU:1, one launch (start us, length us, event | category | flops | bytes accessed | tf_op | source)
XLA Modules:
  0.0 115.6 jit_solution(6183174452507895478)
XLA Ops:
  0.6 113.3 %shard_map.122 = (bf16[64,1024]{1,0:T(8,128)(2,1)}, f32[1,512]{1,0:T(1,128)}) custom-call(bf16[64,1024]{1,0:T(8,128)(2,1)} %embed_in.1, bf16[1,135,128,128]{3,2,1,0:T(8,128)(2,1)} %weight_hbm.1, s32[1,135]{1,0:T(1,128)} %tile_rows_in.1, s32[1,135]{1,0:T(1,128)} %tile_cols_in.1, s32[1,128]{1,0:T(1,128)} %send_rows_in.1, s32[1,512]{1,0:T(1,128)} %bitcast.8, ...), custom_call_target="tpu_custom_call" | custom-call | tf_op jit(solution)/shard_map/pallas_call | solution.py:542
  114.0 1.6 %shard_map.123 = (bf16[64,1024]{1,0:T(8,128)(2,1)}, f32[1,512]{1,0:T(1,128)}) custom-call(bf16[64,1024]{1,0:T(8,128)(2,1)} %get-tuple-element.6.out_in, f32[1,512]{1,0:T(1,128)} %get-tuple-element.7.scores_in), custom_call_target="tpu_custom_call" | custom-call | tf_op jit(solution)/shard_map/pallas_call | solution.py:559
